TPU v7x, 128 devices: a whole 4x4x4 slice. The times are simulated.
128 devices in a mesh: blk: 128 (over x, z, y, core).
Axes of the slice: x: 4, y: 4, z: 4, core: 2. Of those that a mesh axis runs over, the one named last changes fastest.
Arguments:
- estimate: float32 [128, 110592], P('blk'), may hold values from 0.3 to 1.5
- observed: bfloat16 [128, 6, 110592], P('blk'), may hold values from 0.19921875 to 2
- psf_cells: float32 [128, 6, 4913], P('blk'), may hold values from 0.005 to 1.8, as said below
- tissue: int32 [128], P('blk'), may hold values from 0 to 1, as said below
- neighbours: int32 [128, 6], P('blk'), may hold values from -1 to 127, as said below
- psf_list: int32 [128, 6, 2], P('blk'), may hold values from 0 to 127
- psf_blend: float32 [128, 6, 2], P('blk'), may hold values from 0.1 to 1
- cell_row: int32 [128], replicated, may hold values from 0 to 127, each once
- view_order: int32 [6], replicated, may hold values from 0 to 5, each once
Outputs:
- refined: float32 [128, 110592], P('blk')
Inputs may be any that keep to these rules, and one draw needn't show every extreme that they name: Block b sits on device b; blocks 0 to 1 and 64 to 65 are always tissue. With h the top bit of a block's number and r the number without it: bit 3j of r is bit j of the first grid coordinate, bit 3j + 1 of the second, bit 3j + 2 is bit j + 1 of the third, whose lowest bit is h. neighbours[b, f] is the block next to b across face f in that grid if both are tissue, else -1. `cell_row`: each grid cell in exactly one row. `view_order`: each view once; the first 2 entries are used. `psf_cells`: Positive.
All inputs are finite; a program needn't handle non-finite values.
Results may differ from a plain program's by a relative error of at most 0.0003.
Values may be sent and summed in bfloat16 or wider, within the bound.
A program may use at most 128 MiB of HBM per device.

v0:
```python
import functools
import math

import jax
import jax.numpy as jnp
import numpy as np
from jax import lax
from jax.experimental import pallas as pl
from jax.experimental.pallas import tpu as pltpu
from jax.sharding import PartitionSpec as P

E = 48
MARGIN = 8
UPDATES = 2
PAD = 64
KS = 17
E3 = 110592
KS3 = 4913
HALF = 24
PLANES = 40
TAPROWS = 32

F32 = jnp.float32
BF16 = jnp.bfloat16


def split_np(table):
    hi = np.asarray(table, np.float32).astype(jnp.bfloat16)
    lo = (np.asarray(table, np.float64) - hi.astype(np.float64)).astype(np.float32).astype(jnp.bfloat16)
    return hi, lo


def lane_table(table):
    hi, lo = split_np(table)
    row = np.concatenate([hi, lo], axis=1)
    return np.concatenate([row, row], axis=0)


def row_table(table):
    hi, lo = split_np(table)
    return np.concatenate([hi, hi, lo, lo], axis=1)


def make_tables():
    step = 2.0 * math.pi / PAD
    k = np.arange(PAD)
    ang = (k[:, None] * k[None, :] % PAD) * step
    cos, sin = np.cos(ang), np.sin(ang)
    fwd_z = np.block([[cos, -sin], [sin, cos]])
    inv_z = np.block([[cos, sin], [-sin, cos]]) / PAD
    fwd_y = np.concatenate([cos, sin], axis=0)
    inv_y = np.concatenate([cos[MARGIN : MARGIN + E], sin[MARGIN : MARGIN + E]], axis=0) / PAD
    t = np.arange(KS) - MARGIN
    ang_t = (t[:, None] * k[None, :]) % PAD * step
    tap_z = np.zeros((128, 128))
    tap_z[:KS, :PAD] = np.cos(ang_t)
    tap_z[:KS, PAD:] = -np.sin(ang_t)
    tap_y = np.zeros((128, TAPROWS))
    tap_y[:PAD, :KS] = np.cos(ang_t).T
    tap_y[PAD:, :KS] = np.sin(ang_t).T
    pack = np.zeros((2, 8 * 128, 128), np.float32)
    place = np.zeros((2, 128, 8 * 128), np.float32)
    for p in range(8):
        for s in range(2):
            for z in range(MARGIN):
                slot = p * 16 + s * 8 + z
                pack[0, p * 128 + s * 64 + MARGIN + z, slot] = 1
                pack[1, p * 128 + s * 64 + E + z, slot] = 1
                place[0, slot, p * 128 + s * 64 + z] = 1
                place[1, slot, p * 128 + s * 64 + MARGIN + E + z] = 1
    return dict(
        fwd_z=lane_table(fwd_z),
        inv_z=lane_table(inv_z),
        tap_z=lane_table(tap_z),
        fwd_y=row_table(fwd_y),
        inv_y=row_table(inv_y),
        tap_y=row_table(tap_y),
        pack=pack.astype(jnp.bfloat16),
        place=place.astype(jnp.bfloat16),
    )


TABLES = make_tables()


def split(values):
    hi = values.astype(BF16)
    lo = (values - hi.astype(F32)).astype(BF16)
    return hi, lo


def low_lanes(shape):
    return lax.broadcasted_iota(jnp.int32, shape, len(shape) - 1) < 64


def lane_sign(shape):
    return jnp.where(low_lanes(shape), 1.0, -1.0).astype(F32)


def dot(a, b):
    return lax.dot_general(a, b, (((1,), (0,)), ((), ())), preferred_element_type=F32)


def lanes_dft(rows, table):
    hi, lo = split(rows)
    both = dot(jnp.concatenate([hi, lo], axis=1), table)
    return both[:, :128] + both[:, 128:]


def rows_dft(planes, table, count, inverse):
    sign = lane_sign((count, 128))
    if inverse:
        sign = -sign
    out = []
    for a in range(0, len(planes), 2):
        cols = []
        for plane in planes[a : a + 2]:
            hi, lo = split(plane)
            cols.append(jnp.concatenate([hi, lo, hi, lo], axis=0))
        rhs = jnp.concatenate(cols, axis=1) if len(cols) > 1 else cols[0]
        both = dot(table, rhs)
        for b in range(len(cols)):
            c_part = both[:count, b * 128 : (b + 1) * 128]
            s_part = both[count : 2 * count, b * 128 : (b + 1) * 128]
            out.append(c_part + sign * pltpu.roll(s_part, 64, 1))
    return out


def emit_faces(cp_ref, pack_ref, faces):
    xm_ref, xp_ref, ym_ref, yp_ref, zm_ref, zp_ref = faces
    xm_ref[...] = cp_ref[0:8].reshape(8 * E, 128).astype(BF16)
    xp_ref[...] = cp_ref[16:24].reshape(8 * E, 128).astype(BF16)
    ym_ref[...] = cp_ref[:, 0:8, :].reshape(HALF * 8, 128).astype(BF16)
    yp_ref[...] = cp_ref[:, E - 8 : E, :].reshape(HALF * 8, 128).astype(BF16)
    for g in range(3):
        wide = jnp.concatenate([cp_ref[g * 8 + p].astype(BF16) for p in range(8)], axis=1)
        zm_ref[g * E : (g + 1) * E, :] = dot(wide, pack_ref[0]).astype(BF16)
        zp_ref[g * E : (g + 1) * E, :] = dot(wide, pack_ref[1]).astype(BF16)


FACE_SHAPES = [(8 * E, 128), (8 * E, 128), (HALF * 8, 128), (HALF * 8, 128), (3 * E, 128), (3 * E, 128)]


def start_kernel(est_ref, pack_ref, cp_ref, *faces):
    def body(o, carry):
        cp_ref[o] = est_ref[o] + pltpu.roll(est_ref[o + HALF], 64, 1)
        return carry

    lax.fori_loop(0, HALF, body, 0)
    emit_faces(cp_ref, pack_ref, faces)


def forward_planes(src_ref, z_ref, spec_ref, rows, fwd_z, fwd_y):
    group = 8

    def z_body(it, carry):
        block = src_ref[pl.ds(it * group, group)].reshape(group * rows, 128)
        z_ref[pl.ds(it * group, group), 0:rows, :] = lanes_dft(block, fwd_z).reshape(group, rows, 128)
        return carry

    lax.fori_loop(0, PLANES // group, z_body, 0)

    def y_body(it, carry):
        planes = [z_ref[it * group + j, 0:rows, :] for j in range(group)]
        for j, plane in enumerate(rows_dft(planes, fwd_y, PAD, False)):
            spec_ref[it * group + j] = plane
        return carry

    lax.fori_loop(0, PLANES // group, y_body, 0)


def filter_planes(spec_ref, kr_ref, ki_ref, out_ref, conjugate):
    group = 4
    sign = lane_sign((8, 128))
    if not conjugate:
        sign = -sign

    def body(it, carry):
        kb = it // (HALF // group)
        og = it % (HALF // group)
        rows = pl.ds(pl.multiple_of(kb * 8, 8), 8)
        first = og * group
        acc_r = [jnp.zeros((8, 128), F32) for _ in range(group)]
        acc_i = [jnp.zeros((8, 128), F32) for _ in range(group)]
        for m in range(group + KS - 1):
            value = spec_ref[first + m, rows, :]
            for j in range(group):
                d = m - j
                if 0 <= d < KS:
                    tap = d if conjugate else KS - 1 - d
                    acc_r[j] = acc_r[j] + kr_ref[tap, rows, :] * value
                    acc_i[j] = acc_i[j] + ki_ref[tap, rows, :] * value
        for j in range(group):
            out_ref[first + j, rows, :] = acc_r[j] + sign * pltpu.roll(acc_i[j], 64, 1)
        return carry

    lax.fori_loop(0, 8 * (HALF // group), body, 0)


def inverse_planes(spec_ref, y_ref, out_ref, inv_y, inv_z):
    group = 8

    def y_body(it, carry):
        planes = [spec_ref[it * group + j] for j in range(group)]
        for j, plane in enumerate(rows_dft(planes, inv_y, E, True)):
            y_ref[it * group + j, 0:E, :] = plane
        return carry

    lax.fori_loop(0, HALF // group, y_body, 0)

    def z_body(it, carry):
        block = y_ref[pl.ds(it * group, group), 0:E, :].reshape(group * E, 128)
        out_ref[pl.ds(it * group, group)] = lanes_dft(block, inv_z).reshape(group, E, 128)
        return carry

    lax.fori_loop(0, HALF // group, z_body, 0)


def update_kernel(
    last,
    flags_ref,
    cp_ref,
    obs_ref,
    taps_ref,
    hxm_ref,
    hxp_ref,
    hym_ref,
    hyp_ref,
    hzm_ref,
    hzp_ref,
    fwd_z_ref,
    inv_z_ref,
    tap_z_ref,
    fwd_y_ref,
    fwd_yc_ref,
    inv_y_ref,
    tap_y_ref,
    pack_ref,
    place_ref,
    *refs,
):
    if last:
        out_ref, refs = refs[0], refs[1:]
        faces = ()
    else:
        new_ref, faces, refs = refs[0], refs[1:7], refs[7:]
    ext_ref, pp_ref, z_ref, spec_ref, kr_ref, ki_ref, fil_ref, core_ref, q_ref = refs
    low_core = low_lanes((E, 128))
    low_full = low_lanes((PAD, 128))

    def tap_body(d, carry):
        zt = lanes_dft(taps_ref[d], tap_z_ref[...])
        spec = rows_dft([zt], tap_y_ref[...], PAD, False)[0]
        other = pltpu.roll(spec, 64, 1)
        kr_ref[d] = jnp.where(low_full, spec, other)
        ki_ref[d] = jnp.where(low_full, other, spec)
        return carry

    lax.fori_loop(0, KS, tap_body, 0)

    def face(ref, f):
        return ref[...].astype(F32) * flags_ref[1 + f].astype(F32)

    ext_ref[:, 0:8, :] = face(hym_ref, 2).reshape(HALF, 8, 128)
    ext_ref[:, 56:64, :] = face(hyp_ref, 3).reshape(HALF, 8, 128)
    flag_zm = flags_ref[5].astype(F32)
    flag_zp = flags_ref[6].astype(F32)
    for g in range(3):
        zm = dot(hzm_ref[g * E : (g + 1) * E, :], place_ref[0])
        zp = dot(hzp_ref[g * E : (g + 1) * E, :], place_ref[1])
        for p in range(8):
            lanes = slice(p * 128, (p + 1) * 128)
            ext_ref[g * 8 + p, 8:56, :] = cp_ref[g * 8 + p] + flag_zm * zm[:, lanes] + flag_zp * zp[:, lanes]
    xm = face(hxm_ref, 0).reshape(8, E, 128)
    xp = face(hxp_ref, 1).reshape(8, E, 128)
    pp_ref[8:32] = ext_ref[...]
    for j in range(8):
        for rows in (slice(0, 8), slice(56, 64)):
            near = ext_ref[16 + j, rows, :]
            pp_ref[j, rows, :] = pltpu.roll(jnp.where(low_lanes((8, 128)), near, 0.0), 64, 1)
            near = ext_ref[j, rows, :]
            pp_ref[32 + j, rows, :] = pltpu.roll(jnp.where(low_lanes((8, 128)), 0.0, near), 64, 1)
        pp_ref[j, 8:56, :] = pltpu.roll(jnp.where(low_core, ext_ref[16 + j, 8:56, :], xm[j]), 64, 1)
        pp_ref[32 + j, 8:56, :] = pltpu.roll(jnp.where(low_core, xp[j], ext_ref[j, 8:56, :]), 64, 1)

    forward_planes(pp_ref, z_ref, spec_ref, PAD, fwd_z_ref[...], fwd_y_ref[...])
    filter_planes(spec_ref, kr_ref, ki_ref, fil_ref, False)
    inverse_planes(fil_ref, z_ref, core_ref, inv_y_ref[...], inv_z_ref[...])

    lane = lax.broadcasted_iota(jnp.int32, (E, 128), 1) % 64
    inside = (lane >= MARGIN) & (lane < MARGIN + E)

    def ratio_body(o, carry):
        seen = obs_ref[o].astype(F32) + pltpu.roll(obs_ref[o + HALF].astype(F32), 64, 1)
        q_ref[o + 8] = jnp.where(inside, seen / jnp.where(inside, core_ref[o], 1.0), 0.0)
        return carry

    lax.fori_loop(0, HALF, ratio_body, 0)
    for j in range(8):
        q_ref[j] = pltpu.roll(jnp.where(low_core, q_ref[24 + j], 0.0), 64, 1)
        q_ref[32 + j] = pltpu.roll(jnp.where(low_core, 0.0, q_ref[8 + j]), 64, 1)

    forward_planes(q_ref, z_ref, spec_ref, E, fwd_z_ref[...], fwd_yc_ref[...])
    filter_planes(spec_ref, kr_ref, ki_ref, fil_ref, True)
    inverse_planes(fil_ref, z_ref, core_ref, inv_y_ref[...], inv_z_ref[...])

    alive = flags_ref[0] > 0

    def finish(o, carry):
        old = cp_ref[o]
        new = jnp.where(jnp.logical_and(inside, alive), old * core_ref[o], old)
        if last:
            out_ref[o] = new
            out_ref[o + HALF] = pltpu.roll(new, 64, 1)
        else:
            new_ref[o] = new
        return carry

    lax.fori_loop(0, HALF, finish, 0)
    if not last:
        emit_faces(new_ref, pack_ref, faces)


VMEM = pl.BlockSpec(memory_space=pltpu.VMEM)
SMEM = pl.BlockSpec(memory_space=pltpu.SMEM)


def start_call(est):
    return pl.pallas_call(
        start_kernel,
        out_shape=[jax.ShapeDtypeStruct((HALF, E, 128), F32)]
        + [jax.ShapeDtypeStruct(s, BF16) for s in FACE_SHAPES],
        in_specs=[VMEM] * 2,
        out_specs=[VMEM] * 7,
        name="start",
    )(est, jnp.asarray(TABLES["pack"]))


def fwd_y_core():
    full = TABLES["fwd_y"]
    return np.concatenate([full[:, s * PAD + MARGIN : s * PAD + MARGIN + E] for s in range(4)], axis=1)


def update_call(last, flags, cp, obs, taps, halos):
    if last:
        out_shape = jax.ShapeDtypeStruct((E, E, 128), F32)
        out_specs = VMEM
    else:
        out_shape = [jax.ShapeDtypeStruct((HALF, E, 128), F32)] + [
            jax.ShapeDtypeStruct(s, BF16) for s in FACE_SHAPES
        ]
        out_specs = [VMEM] * 7
    tables = [
        TABLES["fwd_z"],
        TABLES["inv_z"],
        TABLES["tap_z"],
        TABLES["fwd_y"],
        fwd_y_core(),
        TABLES["inv_y"],
        TABLES["tap_y"],
        TABLES["pack"],
        TABLES["place"],
    ]
    return pl.pallas_call(
        functools.partial(update_kernel, last),
        out_shape=out_shape,
        in_specs=[SMEM] + [VMEM] * (9 + len(tables)),
        out_specs=out_specs,
        scratch_shapes=[
            pltpu.VMEM((HALF, PAD, 128), F32),
            pltpu.VMEM((PLANES, PAD, 128), F32),
            pltpu.VMEM((PLANES, PAD, 128), F32),
            pltpu.VMEM((PLANES, PAD, 128), F32),
            pltpu.VMEM((KS, PAD, 128), F32),
            pltpu.VMEM((KS, PAD, 128), F32),
            pltpu.VMEM((HALF, PAD, 128), F32),
            pltpu.VMEM((HALF, E, 128), F32),
            pltpu.VMEM((PLANES, E, 128), F32),
        ],
        name="update_last" if last else "update",
    )(flags, cp, obs, taps, *halos, *[jnp.asarray(t) for t in tables])


GRID = (4, 4, 8)


def coords_of(b):
    return (
        b % 2 + 2 * ((b // 8) % 2),
        (b // 2) % 2 + 2 * ((b // 16) % 2),
        (b // 64) % 2 + 2 * ((b // 4) % 2) + 4 * ((b // 32) % 2),
    )


def block_at(c):
    return (
        c[0] % 2 + 2 * (c[1] % 2) + 4 * ((c[2] // 2) % 2) + 8 * (c[0] // 2) + 16 * (c[1] // 2)
        + 32 * (c[2] // 4) + 64 * (c[2] % 2)
    )


def neighbour_of(b, axis, step):
    c = list(coords_of(b))
    c[axis] = (c[axis] + step + GRID[axis]) % GRID[axis]
    return block_at(c)


MESH = pl.DeviceIdType.MESH
NEAR = 8
FAR = 16
CELLROWS = 40


def greet(peers):
    barrier = pltpu.get_barrier_semaphore()
    for peer in peers:
        pl.semaphore_signal(barrier, inc=1, device_id=(peer,), device_id_type=MESH)
    pl.semaphore_wait(barrier, len(peers))


def near_peers(me):
    base = me // NEAR * NEAR
    return [base + (me % NEAR + s) % NEAR for s in range(1, NEAR)]


def far_peers(me):
    return [(me // NEAR + s) % FAR * NEAR + me % NEAR for s in range(1, FAR)]


def face_peers(me):
    return [neighbour_of(me, f // 2, -1 if f % 2 == 0 else 1) for f in range(6)]


def face_copies(faces, halos, peers, send, recv):
    return [
        pltpu.make_async_remote_copy(
            src_ref=faces[f],
            dst_ref=halos[f ^ 1],
            send_sem=send.at[f],
            recv_sem=recv.at[f],
            device_id=(peers[f],),
            device_id_type=MESH,
        )
        for f in range(6)
    ]


def gather_kernel(cells_ref, weights_ref, *refs):
    faces, refs = refs[:6], refs[6:]
    cells_out, weights_out, halos, refs = refs[0], refs[1], refs[2:8], refs[8:]
    own_sem, near_send, near_recv, far_send, far_recv, face_send, face_recv = refs
    me = lax.axis_index("blk")
    near, far, across = near_peers(me), far_peers(me), face_peers(me)
    greet(near + far + across)
    copies = []
    for s, peer in enumerate(near):
        copies.append(
            pltpu.make_async_remote_copy(
                src_ref=cells_ref,
                dst_ref=cells_out.at[me % NEAR],
                send_sem=near_send.at[s],
                recv_sem=near_recv.at[s],
                device_id=(peer,),
                device_id_type=MESH,
            )
        )
    for s, peer in enumerate(far):
        copies.append(
            pltpu.make_async_remote_copy(
                src_ref=weights_ref,
                dst_ref=weights_out.at[me // NEAR],
                send_sem=far_send.at[s],
                recv_sem=far_recv.at[s],
                device_id=(peer,),
                device_id_type=MESH,
            )
        )
    copies += face_copies(faces, halos, across, face_send, face_recv)
    copies.append(pltpu.make_async_copy(cells_ref, cells_out.at[me % NEAR], own_sem.at[0]))
    copies.append(pltpu.make_async_copy(weights_ref, weights_out.at[me // NEAR], own_sem.at[1]))
    for copy in copies:
        copy.start()
    for copy in copies:
        copy.wait()


def blend_kernel(cell_row_ref, cells_ref, weights_ref, out_ref, scaled_ref):
    me = lax.axis_index("blk")
    base = me // NEAR * NEAR
    row = base + lax.broadcasted_iota(jnp.int32, (NEAR, 128), 0)
    pick = (cell_row_ref[...] == row).astype(F32)
    for a in range(NEAR):
        for u in range(UPDATES):
            rows = slice(u * CELLROWS, (u + 1) * CELLROWS)
            cell = cells_ref[a, rows, :]
            total = jnp.sum(jnp.sum(cell, axis=0, keepdims=True), axis=1, keepdims=True)
            scaled_ref[a, rows, :] = cell / total

    def body(dest, carry):
        for u in range(UPDATES):
            rows = slice(u * CELLROWS, (u + 1) * CELLROWS)
            share = jnp.sum(weights_ref[dest, u : u + 1, :] * pick, axis=1, keepdims=True)
            total = share[0:1, :] * scaled_ref[0, rows, :]
            for a in range(1, NEAR):
                total = total + share[a : a + 1, :] * scaled_ref[a, rows, :]
            out_ref[dest, rows, :] = total
        return carry

    lax.fori_loop(0, FAR, body, 0)


def collect_kernel(parts_ref, out_ref, held_ref, send, recv):
    me = lax.axis_index("blk")
    far = far_peers(me)
    greet(far)
    copies = []
    for s, peer in enumerate(far):
        copies.append(
            pltpu.make_async_remote_copy(
                src_ref=parts_ref.at[(me // NEAR + 1 + s) % FAR],
                dst_ref=held_ref.at[s],
                send_sem=send.at[s],
                recv_sem=recv.at[s],
                device_id=(peer,),
                device_id_type=MESH,
            )
        )
    for copy in copies:
        copy.start()
    total = parts_ref[me // NEAR]
    for s, copy in enumerate(copies):
        copy.wait()
        total = total + held_ref[s]
    out_ref[...] = total


def faces_kernel(*refs):
    faces, halos, (send, recv) = refs[:6], refs[6:12], refs[12:]
    across = face_peers(lax.axis_index("blk"))
    greet(across)
    copies = face_copies(faces, halos, across, send, recv)
    for copy in copies:
        copy.start()
    for copy in copies:
        copy.wait()


HALO_SHAPES = [jax.ShapeDtypeStruct(FACE_SHAPES[f ^ 1], BF16) for f in range(6)]
DMA = pltpu.SemaphoreType.DMA
ROWS = UPDATES * CELLROWS


def gather_call(cells, weights, faces):
    result = pl.pallas_call(
        gather_kernel,
        out_shape=[
            jax.ShapeDtypeStruct((NEAR, ROWS, 128), F32),
            jax.ShapeDtypeStruct((FAR, 8, 128), F32),
        ]
        + HALO_SHAPES,
        in_specs=[VMEM] * 8,
        out_specs=[VMEM] * 8,
        scratch_shapes=[
            DMA((2,)),
            DMA((NEAR - 1,)),
            DMA((NEAR - 1,)),
            DMA((FAR - 1,)),
            DMA((FAR - 1,)),
            DMA((6,)),
            DMA((6,)),
        ],
        compiler_params=pltpu.CompilerParams(collective_id=0, has_side_effects=True),
        name="gather",
    )(cells, weights, *faces)
    return result[0], result[1], result[2:]


def blend_call(cell_row, cells, weights):
    return pl.pallas_call(
        blend_kernel,
        out_shape=jax.ShapeDtypeStruct((FAR, ROWS, 128), F32),
        in_specs=[VMEM] * 3,
        out_specs=VMEM,
        scratch_shapes=[pltpu.VMEM((NEAR, ROWS, 128), F32)],
        name="blend",
    )(cell_row.reshape(1, 128), cells, weights)


def collect_call(parts):
    return pl.pallas_call(
        collect_kernel,
        out_shape=jax.ShapeDtypeStruct((ROWS, 128), F32),
        in_specs=[VMEM],
        out_specs=VMEM,
        scratch_shapes=[pltpu.VMEM((FAR - 1, ROWS, 128), F32), DMA((FAR - 1,)), DMA((FAR - 1,))],
        compiler_params=pltpu.CompilerParams(collective_id=1, has_side_effects=True),
        name="collect",
    )(parts)


def faces_call(faces):
    return pl.pallas_call(
        faces_kernel,
        out_shape=HALO_SHAPES,
        in_specs=[VMEM] * 6,
        out_specs=[VMEM] * 6,
        scratch_shapes=[DMA((6,)), DMA((6,))],
        compiler_params=pltpu.CompilerParams(collective_id=2, has_side_effects=True),
        name="faces",
    )(*faces)


def local(
    estimate, observed, psf_cells, tissue, neighbours, psf_list, psf_blend, cell_row, view_order
):
    flags = jnp.concatenate([tissue, (neighbours[0] >= 0).astype(jnp.int32)])
    est = jnp.pad(estimate.reshape(E, E, E), ((0, 0), (0, 0), (8, 72)))
    views = view_order[:UPDATES]
    lists = psf_list[0][views]
    blend = psf_blend[0][views]
    blend = blend / jnp.sum(blend, axis=1, keepdims=True)
    number = jnp.arange(128, dtype=jnp.int32)
    weights = jnp.sum(
        jnp.where(lists[:, :, None] == number[None, None, :], blend[:, :, None], 0.0), axis=1
    )
    weights = jnp.pad(weights, ((0, 8 - UPDATES), (0, 0)))
    cells = jnp.concatenate(
        [
            lax.dynamic_index_in_dim(psf_cells[0], view_order[u], 0, keepdims=False)
            for u in range(UPDATES)
        ]
    ).reshape(UPDATES, KS3)
    cells = jnp.pad(cells, ((0, 0), (0, CELLROWS * 128 - KS3))).reshape(ROWS, 128)
    seen = []
    for update in range(UPDATES):
        obs = lax.dynamic_index_in_dim(observed, view_order[update], 1, keepdims=False)
        seen.append(jnp.pad(obs.reshape(E, E, E), ((0, 0), (0, 0), (8, 72))))
    cp, *faces = start_call(est)
    gathered, shares, halos = gather_call(cells, weights, faces)
    kernel = collect_call(blend_call(cell_row, gathered, shares))
    taps = kernel.reshape(UPDATES, CELLROWS * 128)[:, :KS3].reshape(UPDATES, KS, KS, KS)
    taps = jnp.pad(taps, ((0, 0), (0, 0), (0, TAPROWS - KS), (0, 128 - KS)))
    cp, *faces = update_call(False, flags, cp, seen[0], taps[0], halos)
    halos = faces_call(faces)
    result = update_call(True, flags, cp, seen[1], taps[1], halos)
    return result[:, :, 8:56].reshape(1, E3)


def solution(mesh):
    return jax.shard_map(
        local,
        mesh=mesh,
        in_specs=(
            P("blk", None),
            P("blk", None, None),
            P("blk", None, None),
            P("blk"),
            P("blk", None),
            P("blk", None, None),
            P("blk", None, None),
            P(),
            P(),
        ),
        out_specs=P("blk", None),
        check_vma=False,
    )
```

profile of v0, /device:TPU:0, one launch (start us, length us, event | category | flops | bytes accessed | tf_op | source)
XLA Modules:
  0.0 144.4 jit_solution(14951425251897552301)
XLA Ops:
  0.0 1.4 fusion.4
  5.4 0.8 dynamic-slice_reduce_fusion.3
  6.3 0.1 reshape.59
  6.5 0.7 reshape.60.cells_ref
  7.1 0.5 broadcast.55
  7.6 2.7 %reduce.12 = f32[110592]{0:T(1024)S(1)} reduce(f32[1,110592]{1,0:T(1,128)} %param.19, f32[]{:T(128)} %broadcast.55), dimensions={0}, to_apply=%param.19.reduce_sub_computation.3 | reduce | bytes 884740 | tf_op args[0]
  10.4 0.4 reshape.56
  10.8 1.4 pad.23.est_ref
  12.2 4.2 %start.1 = (f32[24,48,128]{2,1,0:T(8,128)}, bf16[384,128]{1,0:T(8,128)(2,1)}, bf16[384,128]{1,0:T(8,128)(2,1)}, bf16[192,128]{1,0:T(8,128)(2,1)}, bf16[192,128]{...) custom-call(f32[48,48,128]{2,1,0:T(8,128)} %pad.23.est_ref, ...), custom_call_target="tpu_custom_call" | custom-call | tf_op jit(solution)/shard_map/start/pallas_call | solution.py:329
  16.5 0.1 copy.25
  16.5 0.6 gather_fusion.1
  17.1 0.1 reduce_sum.18
  17.3 0.1 copy.24
  17.4 0.6 gather_fusion
  18.1 0.6 pad.26.weights_ref
  18.7 18.9 %gather.13 = (f32[8,80,128]{2,1,0:T(8,128)}, f32[16,8,128]{2,1,0:T(8,128)}, bf16[384,128]{1,0:T(8,128)(2,1)}, bf16[384,128]{1,0:T(8,128)(2,1)}, bf16[192,128]{1,...) custom-call(f32[80,128]{1,0:T(8,128)} %reshape.60.cells_ref, ...), custom_call_target="tpu_custom_call" | custom-call | tf_op jit(solution)/shard_map/gather/pallas_call | solution.py:554
  37.5 3.6 %blend.1.parts_ref = f32[16,80,128]{2,1,0:T(8,128)} custom-call(s32[1,128]{1,0:T(1,128)} %bitcast.13, f32[8,80,128]{2,1,0:T(8,128)} %get-tuple-element.40.cells_ref, f32[16,8,128]{2,1,0:T(8,128)} %get-tuple-element.41.weights_ref), custom_call_target="tpu_custom_call" | custom-call | tf_op jit(solution)/shard_map/blend/pallas_call | solution.py:579
  41.1 13.7 %collect.1 = f32[80,128]{1,0:T(8,128)} custom-call(f32[16,80,128]{2,1,0:T(8,128)} %blend.1.parts_ref), custom_call_target="tpu_custom_call" | custom-call | tf_op jit(solution)/shard_map/collect/pallas_call | solution.py:590
  54.8 0.8 reshape.61
  55.6 0.2 reshape.62
  55.9 0.9 fusion.1
  56.7 2.6 %dynamic-slice_reduce_fusion = (bf16[110592]{0:T(1024)(128)(2,1)S(1)}, bf16[110592]{0:T(1024)(128)(2,1)S(1)}) fusion(bf16[1,6,110592]{2,1,0:T(8,128)(2,1)S(1)} %copy-done, s32[]{:T(128)S(6)} %select_n.19, s32[]{:T(128)S(6)} %select_n.18), kind=kLoop, calls=%fused_computation.4 | loop fusion | bytes 884744 | tf_op jit(solution)/shard_map/jit(dynamic_index_in_dim)/dynamic_slice | solution.py:636
  59.3 0.5 reshape.57
  59.9 1.0 pad.24.obs_ref
  61.6 0.6 pad_add_fusion.flags_ref
  62.2 32.6 %update.1 = (f32[24,48,128]{2,1,0:T(8,128)}, bf16[384,128]{1,0:T(8,128)(2,1)}, bf16[384,128]{1,0:T(8,128)(2,1)}, bf16[192,128]{1,0:T(8,128)(2,1)}, bf16[192,128]...) custom-call(s32[7]{0:T(128)} %pad_add_fusion.flags_ref, f32[24,48,128]{2,1,0:T(8,128)} %get-tuple-element.33.cp_ref, ...), custom_call_target="tpu_custom_call" | custom-call | tf_op jit(solution)/shard_map/update/pallas_call | solution.py:364
  94.8 10.2 %faces.1 = (bf16[384,128]{1,0:T(8,128)(2,1)}, bf16[384,128]{1,0:T(8,128)(2,1)}, bf16[192,128]{1,0:T(8,128)(2,1)}, bf16[192,128]{1,0:T(8,128)(2,1)}, bf16[144,128]{1,0:T(8,128)(2,1)}, /*index=5*/bf16[144,128]{1,0:T(8,128)(2,1)}) custom-call(bf16[384,128]{1,0:T(8,128)(2,1)} %get-tuple-element.49.refs_0_, bf16[384,128]{1,0:T(8,128)(2,1)} %get-tuple-element.50.refs_1_, ...), custom_call_target="tpu_custom_call" | custom-call | tf_op jit(solution)/shard_map/faces/pallas_call | solution.py:602
  104.9 0.5 reshape.63
  105.5 1.0 pad.28.obs_ref
  106.5 34.3 %update_last.1 = f32[48,48,128]{2,1,0:T(8,128)} custom-call(s32[7]{0:T(128)} %pad_add_fusion.flags_ref, f32[24,48,128]{2,1,0:T(8,128)} %get-tuple-element.48.cp_ref, bf16[48,48,128]{2,1,0:T(8,128)(2,1)} %pad.28.obs_ref, f32[17,32,128]{2,1,0:T(8,128)} %get-tuple-element.65.taps_ref, bf16[384,128]{1,0:T(8,128)(2,1)} %get-tuple-element.55.hxm_ref, ...), custom_call_target="tpu_custom_call" | custom-call | tf_op jit(solution)/shard_map/update_last/pallas_call | solution.py:364
  140.8 1.6 %slice.35 = f32[48,48,48]{2,1,0:T(8,128)S(1)} slice(f32[48,48,128]{2,1,0:T(8,128)} %update_last.1), slice={[0:48], [0:48], [8:56]} | slice | bytes 884736 | tf_op jit(solution)/shard_map/slice | solution.py:646
  142.5 1.9 %reshape.64 = f32[1,110592]{1,0:T(1,128)} reshape(f32[48,48,48]{2,1,0:T(8,128)S(1)} %slice.35) | data formatting | bytes 884736 | tf_op jit(solution)/shard_map/reshape | solution.py:646
  (18 shorter events, 0.3 us)
Async XLA Ops:
  12.2 4.2 %copy-start.1 = (s32[6]{0:T(128)S(1)}, s32[6]{0:T(128)}, u32[]{:S(2)}) copy-start(s32[6]{0:T(128)} %param.27) | copy-start | bytes 76
  12.2 4.2 %copy-start.2 = (f32[1,6,2]{1,2,0:T(2,128)S(1)}, f32[1,6,2]{1,2,0:T(2,128)}, u32[]{:S(2)}) copy-start(f32[1,6,2]{1,2,0:T(2,128)} %param.25) | copy-start | bytes 148
  12.2 5.1 %copy-start.3 = (s32[1,6,2]{1,2,0:T(2,128)S(1)}, s32[1,6,2]{1,2,0:T(2,128)}, u32[]{:S(2)}) copy-start(s32[1,6,2]{1,2,0:T(2,128)} %param.24) | copy-start | bytes 148
  41.1 15.6 %copy-start = (bf16[1,6,110592]{2,1,0:T(8,128)(2,1)S(1)}, bf16[1,6,110592]{2,1,0:T(8,128)(2,1)}, u32[]{:S(2)}) copy-start(bf16[1,6,110592]{2,1,0:T(8,128)(2,1)} %param.20) | copy-start | bytes 3981316
  59.3 2.2 %copy-start.4 = (s32[1,6]{1,0:T(1,128)S(1)}, s32[1,6]{1,0:T(1,128)}, u32[]{:S(2)}) copy-start(s32[1,6]{1,0:T(1,128)} %param.23) | copy-start | bytes 76
where the time goes:
time: 145 us; the launch traced here: 144 us
  Pallas kernels  117 us (81%)
  local copies, waits for them, and re-layouts  18.5 us (13%)
  between operations  4.81 us (3%)
  other arithmetic  3.66 us (3%)
    pallas_call x2, Pallas kernels, update_call(): pl.pallas_call(functools.partial(update_kernel, last), out_shape=out_shap...  66.9 us
    pallas_call x1, Pallas kernels, gather_call(): pl.pallas_call(gather_kernel, out_shape=[jax.ShapeDtypeStruct((NEAR, ROWS...  18.9 us
    pallas_call x1, Pallas kernels, collect_call(): pl.pallas_call(collect_kernel, out_shape=jax.ShapeDtypeStruct((ROWS, 128)...  13.7 us
    pallas_call x1, Pallas kernels, faces_call(): pl.pallas_call(faces_kernel, out_shape=HALO_SHAPES, in_specs=[VMEM] * 6,...  10.2 us
    pallas_call x1, Pallas kernels, start_call(): pl.pallas_call(start_kernel, out_shape=[jax.ShapeDtypeStruct((HALF, E, 12...  4.2 us
    pallas_call x1, Pallas kernels, blend_call(): pl.pallas_call(blend_kernel, out_shape=jax.ShapeDtypeStruct((FAR, ROWS, 1...  3.58 us

commit v1 on v0

--- a/solution.py
+++ b/solution.py
@@ -150,19 +150,19 @@
     emit_faces(cp_ref, pack_ref, faces)
 
 
-def forward_planes(src_ref, z_ref, spec_ref, rows, fwd_z, fwd_y):
-    group = 8
+def forward_planes(src_ref, z_ref, spec_ref, rows, fwd_z_ref, fwd_y_ref):
+    group = 20
 
     def z_body(it, carry):
         block = src_ref[pl.ds(it * group, group)].reshape(group * rows, 128)
-        z_ref[pl.ds(it * group, group), 0:rows, :] = lanes_dft(block, fwd_z).reshape(group, rows, 128)
+        z_ref[pl.ds(it * group, group), 0:rows, :] = lanes_dft(block, fwd_z_ref[...]).reshape(group, rows, 128)
         return carry
 
     lax.fori_loop(0, PLANES // group, z_body, 0)
 
     def y_body(it, carry):
         planes = [z_ref[it * group + j, 0:rows, :] for j in range(group)]
-        for j, plane in enumerate(rows_dft(planes, fwd_y, PAD, False)):
+        for j, plane in enumerate(rows_dft(planes, fwd_y_ref[...], PAD, False)):
             spec_ref[it * group + j] = plane
         return carry
 
@@ -170,39 +170,43 @@
 
 
 def filter_planes(spec_ref, kr_ref, ki_ref, out_ref, conjugate):
-    group = 4
+    group = 12
     sign = lane_sign((8, 128))
     if not conjugate:
         sign = -sign
 
-    def body(it, carry):
-        kb = it // (HALF // group)
-        og = it % (HALF // group)
+    def body(kb, carry):
         rows = pl.ds(pl.multiple_of(kb * 8, 8), 8)
-        first = og * group
-        acc_r = [jnp.zeros((8, 128), F32) for _ in range(group)]
-        acc_i = [jnp.zeros((8, 128), F32) for _ in range(group)]
-        for m in range(group + KS - 1):
-            value = spec_ref[first + m, rows, :]
+        for first in range(0, HALF, group):
+            values = {}
+            acc_r, acc_i = [None] * group, [None] * group
+            for d in range(KS):
+                tap = d if conjugate else KS - 1 - d
+                kr = kr_ref[tap, rows, :]
+                ki = ki_ref[tap, rows, :]
+                for j in range(group):
+                    m = first + j + d
+                    if m not in values:
+                        values[m] = spec_ref[m, rows, :]
+                    if d == 0:
+                        acc_r[j] = kr * values[m]
+                        acc_i[j] = ki * values[m]
+                    else:
+                        acc_r[j] = acc_r[j] + kr * values[m]
+                        acc_i[j] = acc_i[j] + ki * values[m]
             for j in range(group):
-                d = m - j
-                if 0 <= d < KS:
-                    tap = d if conjugate else KS - 1 - d
-                    acc_r[j] = acc_r[j] + kr_ref[tap, rows, :] * value
-                    acc_i[j] = acc_i[j] + ki_ref[tap, rows, :] * value
-        for j in range(group):
-            out_ref[first + j, rows, :] = acc_r[j] + sign * pltpu.roll(acc_i[j], 64, 1)
-        return carry
-
-    lax.fori_loop(0, 8 * (HALF // group), body, 0)
-
-
-def inverse_planes(spec_ref, y_ref, out_ref, inv_y, inv_z):
-    group = 8
+                out_ref[first + j, rows, :] = acc_r[j] + sign * pltpu.roll(acc_i[j], 64, 1)
+        return carry
+
+    lax.fori_loop(0, PAD // 8, body, 0)
+
+
+def inverse_planes(spec_ref, y_ref, out_ref, inv_y_ref, inv_z_ref):
+    group = 12
 
     def y_body(it, carry):
         planes = [spec_ref[it * group + j] for j in range(group)]
-        for j, plane in enumerate(rows_dft(planes, inv_y, E, True)):
+        for j, plane in enumerate(rows_dft(planes, inv_y_ref[...], E, True)):
             y_ref[it * group + j, 0:E, :] = plane
         return carry
 
@@ -210,7 +214,7 @@
 
     def z_body(it, carry):
         block = y_ref[pl.ds(it * group, group), 0:E, :].reshape(group * E, 128)
-        out_ref[pl.ds(it * group, group)] = lanes_dft(block, inv_z).reshape(group, E, 128)
+        out_ref[pl.ds(it * group, group)] = lanes_dft(block, inv_z_ref[...]).reshape(group, E, 128)
         return carry
 
     lax.fori_loop(0, HALF // group, z_body, 0)
@@ -248,15 +252,13 @@
     low_core = low_lanes((E, 128))
     low_full = low_lanes((PAD, 128))
 
-    def tap_body(d, carry):
-        zt = lanes_dft(taps_ref[d], tap_z_ref[...])
-        spec = rows_dft([zt], tap_y_ref[...], PAD, False)[0]
+    rows = lanes_dft(taps_ref[...].reshape(KS * TAPROWS, 128), tap_z_ref[...])
+    z_ref[0:KS, 0:TAPROWS, :] = rows.reshape(KS, TAPROWS, 128)
+    planes = [z_ref[d, 0:TAPROWS, :] for d in range(KS)]
+    for d, spec in enumerate(rows_dft(planes, tap_y_ref[...], PAD, False)):
         other = pltpu.roll(spec, 64, 1)
         kr_ref[d] = jnp.where(low_full, spec, other)
         ki_ref[d] = jnp.where(low_full, other, spec)
-        return carry
-
-    lax.fori_loop(0, KS, tap_body, 0)
 
     def face(ref, f):
         return ref[...].astype(F32) * flags_ref[1 + f].astype(F32)
@@ -283,40 +285,42 @@
         pp_ref[j, 8:56, :] = pltpu.roll(jnp.where(low_core, ext_ref[16 + j, 8:56, :], xm[j]), 64, 1)
         pp_ref[32 + j, 8:56, :] = pltpu.roll(jnp.where(low_core, xp[j], ext_ref[j, 8:56, :]), 64, 1)
 
-    forward_planes(pp_ref, z_ref, spec_ref, PAD, fwd_z_ref[...], fwd_y_ref[...])
+    forward_planes(pp_ref, z_ref, spec_ref, PAD, fwd_z_ref, fwd_y_ref)
     filter_planes(spec_ref, kr_ref, ki_ref, fil_ref, False)
-    inverse_planes(fil_ref, z_ref, core_ref, inv_y_ref[...], inv_z_ref[...])
+    inverse_planes(fil_ref, z_ref, core_ref, inv_y_ref, inv_z_ref)
 
     lane = lax.broadcasted_iota(jnp.int32, (E, 128), 1) % 64
     inside = (lane >= MARGIN) & (lane < MARGIN + E)
 
-    def ratio_body(o, carry):
-        seen = obs_ref[o].astype(F32) + pltpu.roll(obs_ref[o + HALF].astype(F32), 64, 1)
-        q_ref[o + 8] = jnp.where(inside, seen / jnp.where(inside, core_ref[o], 1.0), 0.0)
-        return carry
-
-    lax.fori_loop(0, HALF, ratio_body, 0)
+    def ratio_body(it, carry):
+        for o in [it * 4 + j for j in range(4)]:
+            seen = obs_ref[o].astype(F32) + pltpu.roll(obs_ref[o + HALF].astype(F32), 64, 1)
+            q_ref[o + 8] = jnp.where(inside, seen / jnp.where(inside, core_ref[o], 1.0), 0.0)
+        return carry
+
+    lax.fori_loop(0, HALF // 4, ratio_body, 0)
     for j in range(8):
         q_ref[j] = pltpu.roll(jnp.where(low_core, q_ref[24 + j], 0.0), 64, 1)
         q_ref[32 + j] = pltpu.roll(jnp.where(low_core, 0.0, q_ref[8 + j]), 64, 1)
 
-    forward_planes(q_ref, z_ref, spec_ref, E, fwd_z_ref[...], fwd_yc_ref[...])
+    forward_planes(q_ref, z_ref, spec_ref, E, fwd_z_ref, fwd_yc_ref)
     filter_planes(spec_ref, kr_ref, ki_ref, fil_ref, True)
-    inverse_planes(fil_ref, z_ref, core_ref, inv_y_ref[...], inv_z_ref[...])
+    inverse_planes(fil_ref, z_ref, core_ref, inv_y_ref, inv_z_ref)
 
     alive = flags_ref[0] > 0
 
-    def finish(o, carry):
-        old = cp_ref[o]
-        new = jnp.where(jnp.logical_and(inside, alive), old * core_ref[o], old)
-        if last:
-            out_ref[o] = new
-            out_ref[o + HALF] = pltpu.roll(new, 64, 1)
-        else:
-            new_ref[o] = new
-        return carry
-
-    lax.fori_loop(0, HALF, finish, 0)
+    def finish(it, carry):
+        for o in [it * 4 + j for j in range(4)]:
+            old = cp_ref[o]
+            new = jnp.where(jnp.logical_and(inside, alive), old * core_ref[o], old)
+            if last:
+                out_ref[o] = new
+                out_ref[o + HALF] = pltpu.roll(new, 64, 1)
+            else:
+                new_ref[o] = new
+        return carry
+
+    lax.fori_loop(0, HALF // 4, finish, 0)
     if not last:
         emit_faces(new_ref, pack_ref, faces)
 

time: 145 us -> 106 us (0.73)
  Pallas kernels: 117 us -> 78.8 us
    pallas_call x2, Pallas kernels: 66.9 us -> 28.3 us  [update_call(): pl.pallas_call(functools.partial(update_kernel, last), out_shape=out_shap...]
where the time goes in v1:
time: 106 us
  Pallas kernels  78.8 us (74%)
  local copies, waits for them, and re-layouts  18.5 us (17%)
  between operations  4.81 us (5%)
  other arithmetic  3.66 us (3%)
    pallas_call x2, Pallas kernels, update_call(): pl.pallas_call(functools.partial(update_kernel, last), out_shape=out_shap...  28.3 us
    pallas_call x1, Pallas kernels, gather_call(): pl.pallas_call(gather_kernel, out_shape=[jax.ShapeDtypeStruct((NEAR, ROWS...  18.9 us
    pallas_call x1, Pallas kernels, collect_call(): pl.pallas_call(collect_kernel, out_shape=jax.ShapeDtypeStruct((ROWS, 128)...  13.7 us
    pallas_call x1, Pallas kernels, faces_call(): pl.pallas_call(faces_kernel, out_shape=HALO_SHAPES, in_specs=[VMEM] * 6,...  10.2 us
    pallas_call x1, Pallas kernels, start_call(): pl.pallas_call(start_kernel, out_shape=[jax.ShapeDtypeStruct((HALF, E, 12...  4.2 us
    pallas_call x1, Pallas kernels, blend_call(): pl.pallas_call(blend_kernel, out_shape=jax.ShapeDtypeStruct((FAR, ROWS, 1...  3.58 us
    unnamed x1, other arithmetic  2.71 us
    dynamic_slice x1, local copies, waits for them, and re-layouts, local(): lax.dynamic_index_in_dim(observed, view_order[update], 1, keepdims=False)  2.58 us

profile of v1, /device:TPU:0, one launch (start us, length us, event | category | flops | bytes accessed | tf_op | source)
XLA Modules:
  0.0 105.8 jit_solution(16178729664365198035)
XLA Ops:
  0.0 1.4 %fusion.4 = (s32[1]{0:T(128)}, s32[1]{0:T(128)}) fusion(s32[6]{0:T(128)} %param.27), kind=kLoop, calls=%fused_computation.19 | loop fusion | bytes 16 | tf_op jit(solution)/shard_map/slice | solution.py:640
  5.4 0.8 dynamic-slice_reduce_fusion.3
  6.3 0.1 reshape.59
  6.5 0.7 reshape.60.cells_ref
  7.1 0.5 broadcast.55
  7.6 2.7 %reduce.12 = f32[110592]{0:T(1024)S(1)} reduce(f32[1,110592]{1,0:T(1,128)} %param.19, f32[]{:T(128)} %broadcast.55), dimensions={0}, to_apply=%param.19.reduce_sub_computation.3 | reduce | bytes 884740 | tf_op args[0]
  10.4 0.4 reshape.56
  10.8 1.4 %pad.23.est_ref = f32[48,48,128]{2,1,0:T(8,128)} pad(f32[48,48,48]{2,1,0:T(8,128)S(1)} %reshape.56, f32[]{:T(128)} %constant.40.clone.1), padding=0_0x0_0x8_72 | pad | bytes 1622020 | tf_op jit(solution)/shard_map/jit(_pad)/pad | solution.py:621
  12.2 4.2 %start.1 = (f32[24,48,128]{2,1,0:T(8,128)}, bf16[384,128]{1,0:T(8,128)(2,1)}, bf16[384,128]{1,0:T(8,128)(2,1)}, bf16[192,128]{1,0:T(8,128)(2,1)}, bf16[192,128]{...) custom-call(f32[48,48,128]{2,1,0:T(8,128)} %pad.23.est_ref, ...), custom_call_target="tpu_custom_call" | custom-call | tf_op jit(solution)/shard_map/start/pallas_call | solution.py:333
  16.5 0.1 copy.25
  16.5 0.6 gather_fusion.1
  17.1 0.1 reduce_sum.18
  17.3 0.1 copy.24
  17.4 0.6 gather_fusion
  18.1 0.6 pad.26.weights_ref
  18.7 18.9 %gather.13 = (f32[8,80,128]{2,1,0:T(8,128)}, f32[16,8,128]{2,1,0:T(8,128)}, bf16[384,128]{1,0:T(8,128)(2,1)}, bf16[384,128]{1,0:T(8,128)(2,1)}, bf16[192,128]{1,...) custom-call(f32[80,128]{1,0:T(8,128)} %reshape.60.cells_ref, ...), custom_call_target="tpu_custom_call" | custom-call | tf_op jit(solution)/shard_map/gather/pallas_call | solution.py:558
  37.6 3.6 %blend.1.parts_ref = f32[16,80,128]{2,1,0:T(8,128)} custom-call(s32[1,128]{1,0:T(1,128)} %bitcast.13, f32[8,80,128]{2,1,0:T(8,128)} %get-tuple-element.40.cells_ref, f32[16,8,128]{2,1,0:T(8,128)} %get-tuple-element.41.weights_ref), custom_call_target="tpu_custom_call" | custom-call | tf_op jit(solution)/shard_map/blend/pallas_call | solution.py:583
  41.1 13.7 %collect.1 = f32[80,128]{1,0:T(8,128)} custom-call(f32[16,80,128]{2,1,0:T(8,128)} %blend.1.parts_ref), custom_call_target="tpu_custom_call" | custom-call | tf_op jit(solution)/shard_map/collect/pallas_call | solution.py:594
  54.8 0.8 reshape.61
  55.6 0.2 reshape.62
  55.9 0.9 fusion.1
  56.7 2.6 %dynamic-slice_reduce_fusion = (bf16[110592]{0:T(1024)(128)(2,1)S(1)}, bf16[110592]{0:T(1024)(128)(2,1)S(1)}) fusion(bf16[1,6,110592]{2,1,0:T(8,128)(2,1)S(1)} %copy-done, s32[]{:T(128)S(6)} %select_n.19, s32[]{:T(128)S(6)} %select_n.18), kind=kLoop, calls=%fused_computation.4 | loop fusion | bytes 884744 | tf_op jit(solution)/shard_map/jit(dynamic_index_in_dim)/dynamic_slice | solution.py:640
  59.3 0.5 reshape.57
  59.9 1.0 pad.24.obs_ref
  61.6 0.6 pad_add_fusion.flags_ref
  62.2 13.8 %update.1 = (f32[24,48,128]{2,1,0:T(8,128)}, bf16[384,128]{1,0:T(8,128)(2,1)}, bf16[384,128]{1,0:T(8,128)(2,1)}, bf16[192,128]{1,0:T(8,128)(2,1)}, bf16[192,128]...) custom-call(s32[7]{0:T(128)} %pad_add_fusion.flags_ref, f32[24,48,128]{2,1,0:T(8,128)} %get-tuple-element.33.cp_ref, ...), custom_call_target="tpu_custom_call" | custom-call | tf_op jit(solution)/shard_map/update/pallas_call | solution.py:368
  76.0 10.2 %faces.1 = (bf16[384,128]{1,0:T(8,128)(2,1)}, bf16[384,128]{1,0:T(8,128)(2,1)}, bf16[192,128]{1,0:T(8,128)(2,1)}, bf16[192,128]{1,0:T(8,128)(2,1)}, bf16[144,128]{1,0:T(8,128)(2,1)}, /*index=5*/bf16[144,128]{1,0:T(8,128)(2,1)}) custom-call(bf16[384,128]{1,0:T(8,128)(2,1)} %get-tuple-element.49.refs_0_, bf16[384,128]{1,0:T(8,128)(2,1)} %get-tuple-element.50.refs_1_, ...), custom_call_target="tpu_custom_call" | custom-call | tf_op jit(solution)/shard_map/faces/pallas_call | solution.py:606
  86.2 0.5 reshape.63
  86.7 1.0 pad.28.obs_ref
  87.7 14.5 %update_last.1 = f32[48,48,128]{2,1,0:T(8,128)} custom-call(s32[7]{0:T(128)} %pad_add_fusion.flags_ref, f32[24,48,128]{2,1,0:T(8,128)} %get-tuple-element.48.cp_ref, bf16[48,48,128]{2,1,0:T(8,128)(2,1)} %pad.28.obs_ref, f32[17,32,128]{2,1,0:T(8,128)} %get-tuple-element.65.taps_ref, bf16[384,128]{1,0:T(8,128)(2,1)} %get-tuple-element.55.hxm_ref, ...), custom_call_target="tpu_custom_call" | custom-call | tf_op jit(solution)/shard_map/update_last/pallas_call | solution.py:368
  102.2 1.6 %slice.35 = f32[48,48,48]{2,1,0:T(8,128)S(1)} slice(f32[48,48,128]{2,1,0:T(8,128)} %update_last.1), slice={[0:48], [0:48], [8:56]} | slice | bytes 884736 | tf_op jit(solution)/shard_map/slice | solution.py:650
  103.9 1.9 %reshape.64 = f32[1,110592]{1,0:T(1,128)} reshape(f32[48,48,48]{2,1,0:T(8,128)S(1)} %slice.35) | data formatting | bytes 884736 | tf_op jit(solution)/shard_map/reshape | solution.py:650
  (18 shorter events, 0.3 us)
Async XLA Ops:
  12.2 4.2 %copy-start.1 = (s32[6]{0:T(128)S(1)}, s32[6]{0:T(128)}, u32[]{:S(2)}) copy-start(s32[6]{0:T(128)} %param.27) | copy-start | bytes 76
  12.2 4.2 %copy-start.2 = (f32[1,6,2]{1,2,0:T(2,128)S(1)}, f32[1,6,2]{1,2,0:T(2,128)}, u32[]{:S(2)}) copy-start(f32[1,6,2]{1,2,0:T(2,128)} %param.25) | copy-start | bytes 148
  12.2 5.1 %copy-start.3 = (s32[1,6,2]{1,2,0:T(2,128)S(1)}, s32[1,6,2]{1,2,0:T(2,128)}, u32[]{:S(2)}) copy-start(s32[1,6,2]{1,2,0:T(2,128)} %param.24) | copy-start | bytes 148
  41.1 15.6 %copy-start = (bf16[1,6,110592]{2,1,0:T(8,128)(2,1)S(1)}, bf16[1,6,110592]{2,1,0:T(8,128)(2,1)}, u32[]{:S(2)}) copy-start(bf16[1,6,110592]{2,1,0:T(8,128)(2,1)} %param.20) | copy-start | bytes 3981316
  59.3 2.2 %copy-start.4 = (s32[1,6]{1,0:T(1,128)S(1)}, s32[1,6]{1,0:T(1,128)}, u32[]{:S(2)}) copy-start(s32[1,6]{1,0:T(1,128)} %param.23) | copy-start | bytes 76

commit v2 on v1

--- a/solution.py
+++ b/solution.py
@@ -19,6 +19,9 @@
 HALF = 24
 PLANES = 40
 TAPROWS = 32
+
+CELLROWS = 40
+ROWS = UPDATES * CELLROWS
 
 F32 = jnp.float32
 BF16 = jnp.bfloat16
@@ -141,13 +144,74 @@
 FACE_SHAPES = [(8 * E, 128), (8 * E, 128), (HALF * 8, 128), (HALF * 8, 128), (3 * E, 128), (3 * E, 128)]
 
 
-def start_kernel(est_ref, pack_ref, cp_ref, *faces):
-    def body(o, carry):
-        cp_ref[o] = est_ref[o] + pltpu.roll(est_ref[o + HALF], 64, 1)
-        return carry
-
-    lax.fori_loop(0, HALF, body, 0)
+def flat_to_pairs(load, store):
+    for j in range(8):
+        total = None
+        for half in range(2):
+            first = 48 * j
+            k, lane = first // 128, first % 128
+            base = MARGIN + 64 * half
+            value = load(k, half)
+            part = value if lane == base else pltpu.roll(value, (base - lane) % 128, 1)
+            at = lax.broadcasted_iota(jnp.int32, part.shape, 1) - base
+            length = min(48, 128 - lane)
+            picked = jnp.where((at >= 0) & (at < length), part, 0.0)
+            if length < 48:
+                more = pltpu.roll(load(k + 1, half), base + length, 1)
+                picked = jnp.where((at >= length) & (at < 48), more, picked)
+            total = picked if total is None else total + picked
+        store(j, total)
+
+
+def pairs_to_flat(load, store):
+    for half in range(2):
+        for k in range(3):
+            total = None
+            for j in range(8):
+                lane = 48 * j - 128 * k
+                if lane <= -48 or lane >= 128:
+                    continue
+                value = pltpu.roll(load(j), (lane - MARGIN - 64 * half) % 128, 1)
+                at = lax.broadcasted_iota(jnp.int32, value.shape, 1) - lane
+                picked = jnp.where((at >= 0) & (at < 48), value, 0.0)
+                total = picked if total is None else total + picked
+            store(k, half, total)
+
+
+GROUPS = HALF * E // 8
+FLAT = E3 // 128
+
+
+def start_kernel(ints_ref, blend_ref, est_ref, cells_ref, pack_ref, *refs):
+    cp_ref, flat_ref = refs[0], refs[-1]
+    weights_ref, own_ref, faces = refs[1], refs[2], refs[3:9]
+
+    def load(k, half):
+        return est_ref[pl.ds(half * 3 * GROUPS + k, GROUPS, stride=3), :]
+
+    def store(j, rows):
+        flat_ref[pl.ds(j, GROUPS, stride=8), :] = rows
+
+    flat_to_pairs(load, store)
+    cp_ref[...] = flat_ref[...].reshape(HALF, E, 128)
     emit_faces(cp_ref, pack_ref, faces)
+
+    number = lax.broadcasted_iota(jnp.int32, (1, 128), 1)
+    weights_ref[...] = jnp.zeros_like(weights_ref)
+    own_ref[...] = jnp.zeros_like(own_ref)
+    for u in range(UPDATES):
+        view = ints_ref[u]
+        first = jnp.full((1, 128), blend_ref[2 * view], F32)
+        second = jnp.full((1, 128), blend_ref[2 * view + 1], F32)
+        total = first + second
+        weights_ref[u : u + 1, :] = jnp.where(number == ints_ref[6 + 2 * view], first / total, 0.0) + jnp.where(
+            number == ints_ref[7 + 2 * view], second / total, 0.0
+        )
+        for i in range(KS3 // 128):
+            own_ref[u * CELLROWS + i : u * CELLROWS + i + 1, :] = cells_ref[view, :, i * 128 : (i + 1) * 128]
+        tail = KS3 // 128 * 128
+        i = u * CELLROWS + KS3 // 128
+        own_ref[i : i + 1, 0 : KS3 - tail] = cells_ref[view, :, tail:KS3]
 
 
 def forward_planes(src_ref, z_ref, spec_ref, rows, fwd_z_ref, fwd_y_ref):
@@ -248,7 +312,7 @@
         faces = ()
     else:
         new_ref, faces, refs = refs[0], refs[1:7], refs[7:]
-    ext_ref, pp_ref, z_ref, spec_ref, kr_ref, ki_ref, fil_ref, core_ref, q_ref = refs
+    ext_ref, pp_ref, z_ref, spec_ref, kr_ref, ki_ref, fil_ref, core_ref, q_ref, wide_ref, flat_ref = refs
     low_core = low_lanes((E, 128))
     low_full = low_lanes((PAD, 128))
 
@@ -261,18 +325,18 @@
         ki_ref[d] = jnp.where(low_full, other, spec)
 
     def face(ref, f):
-        return ref[...].astype(F32) * flags_ref[1 + f].astype(F32)
+        return jnp.where(flags_ref[19 + f] >= 0, ref[...].astype(F32), 0.0)
 
     ext_ref[:, 0:8, :] = face(hym_ref, 2).reshape(HALF, 8, 128)
     ext_ref[:, 56:64, :] = face(hyp_ref, 3).reshape(HALF, 8, 128)
-    flag_zm = flags_ref[5].astype(F32)
-    flag_zp = flags_ref[6].astype(F32)
+    near_zm = flags_ref[23] >= 0
+    near_zp = flags_ref[24] >= 0
     for g in range(3):
-        zm = dot(hzm_ref[g * E : (g + 1) * E, :], place_ref[0])
-        zp = dot(hzp_ref[g * E : (g + 1) * E, :], place_ref[1])
+        zm = dot(jnp.where(near_zm, hzm_ref[g * E : (g + 1) * E, :].astype(F32), 0.0).astype(BF16), place_ref[0])
+        zp = dot(jnp.where(near_zp, hzp_ref[g * E : (g + 1) * E, :].astype(F32), 0.0).astype(BF16), place_ref[1])
         for p in range(8):
             lanes = slice(p * 128, (p + 1) * 128)
-            ext_ref[g * 8 + p, 8:56, :] = cp_ref[g * 8 + p] + flag_zm * zm[:, lanes] + flag_zp * zp[:, lanes]
+            ext_ref[g * 8 + p, 8:56, :] = cp_ref[g * 8 + p] + zm[:, lanes] + zp[:, lanes]
     xm = face(hxm_ref, 0).reshape(8, E, 128)
     xp = face(hxp_ref, 1).reshape(8, E, 128)
     pp_ref[8:32] = ext_ref[...]
@@ -289,12 +353,23 @@
     filter_planes(spec_ref, kr_ref, ki_ref, fil_ref, False)
     inverse_planes(fil_ref, z_ref, core_ref, inv_y_ref, inv_z_ref)
 
+    wide_ref[...] = obs_ref[...].astype(F32)
+
+    def load_seen(k, half):
+        return wide_ref[pl.ds(half * 3 * GROUPS + k, GROUPS, stride=3), :]
+
+    def store_seen(j, rows):
+        row_ref[pl.ds(j, GROUPS, stride=8), :] = rows
+
+    row_ref = flat_ref.reshape(HALF * E, 128)
+    flat_to_pairs(load_seen, store_seen)
+
     lane = lax.broadcasted_iota(jnp.int32, (E, 128), 1) % 64
     inside = (lane >= MARGIN) & (lane < MARGIN + E)
 
     def ratio_body(it, carry):
         for o in [it * 4 + j for j in range(4)]:
-            seen = obs_ref[o].astype(F32) + pltpu.roll(obs_ref[o + HALF].astype(F32), 64, 1)
+            seen = flat_ref[o]
             q_ref[o + 8] = jnp.where(inside, seen / jnp.where(inside, core_ref[o], 1.0), 0.0)
         return carry
 
@@ -307,15 +382,14 @@
     filter_planes(spec_ref, kr_ref, ki_ref, fil_ref, True)
     inverse_planes(fil_ref, z_ref, core_ref, inv_y_ref, inv_z_ref)
 
-    alive = flags_ref[0] > 0
+    alive = flags_ref[18] > 0
 
     def finish(it, carry):
         for o in [it * 4 + j for j in range(4)]:
             old = cp_ref[o]
             new = jnp.where(jnp.logical_and(inside, alive), old * core_ref[o], old)
             if last:
-                out_ref[o] = new
-                out_ref[o + HALF] = pltpu.roll(new, 64, 1)
+                flat_ref[o] = new
             else:
                 new_ref[o] = new
         return carry
@@ -323,21 +397,36 @@
     lax.fori_loop(0, HALF // 4, finish, 0)
     if not last:
         emit_faces(new_ref, pack_ref, faces)
+        return
+
+    def load_new(j):
+        return row_ref[pl.ds(j, GROUPS, stride=8), :]
+
+    def store_new(k, half, rows):
+        out_ref[pl.ds(half * 3 * GROUPS + k, GROUPS, stride=3), :] = rows
+
+    pairs_to_flat(load_new, store_new)
 
 
 VMEM = pl.BlockSpec(memory_space=pltpu.VMEM)
 SMEM = pl.BlockSpec(memory_space=pltpu.SMEM)
 
 
-def start_call(est):
-    return pl.pallas_call(
+def start_call(ints, blend, est, cells):
+    result = pl.pallas_call(
         start_kernel,
-        out_shape=[jax.ShapeDtypeStruct((HALF, E, 128), F32)]
+        out_shape=[
+            jax.ShapeDtypeStruct((HALF, E, 128), F32),
+            jax.ShapeDtypeStruct((8, 128), F32),
+            jax.ShapeDtypeStruct((ROWS, 128), F32),
+        ]
         + [jax.ShapeDtypeStruct(s, BF16) for s in FACE_SHAPES],
-        in_specs=[VMEM] * 2,
-        out_specs=[VMEM] * 7,
+        in_specs=[SMEM] * 2 + [VMEM] * 3,
+        out_specs=[VMEM] * 9,
+        scratch_shapes=[pltpu.VMEM((HALF * E, 128), F32)],
         name="start",
-    )(est, jnp.asarray(TABLES["pack"]))
+    )(ints, blend, est, cells, jnp.asarray(TABLES["pack"]))
+    return result[0], result[1], result[2], result[3:]
 
 
 def fwd_y_core():
@@ -347,7 +436,7 @@
 
 def update_call(last, flags, cp, obs, taps, halos):
     if last:
-        out_shape = jax.ShapeDtypeStruct((E, E, 128), F32)
+        out_shape = jax.ShapeDtypeStruct((FLAT, 128), F32)
         out_specs = VMEM
     else:
         out_shape = [jax.ShapeDtypeStruct((HALF, E, 128), F32)] + [
@@ -380,6 +469,8 @@
             pltpu.VMEM((HALF, PAD, 128), F32),
             pltpu.VMEM((HALF, E, 128), F32),
             pltpu.VMEM((PLANES, E, 128), F32),
+            pltpu.VMEM((FLAT, 128), F32),
+            pltpu.VMEM((HALF, E, 128), F32),
         ],
         name="update_last" if last else "update",
     )(flags, cp, obs, taps, *halos, *[jnp.asarray(t) for t in tables])
@@ -412,7 +503,6 @@
 MESH = pl.DeviceIdType.MESH
 NEAR = 8
 FAR = 16
-CELLROWS = 40
 
 
 def greet(peers):
@@ -551,7 +641,6 @@
 
 HALO_SHAPES = [jax.ShapeDtypeStruct(FACE_SHAPES[f ^ 1], BF16) for f in range(6)]
 DMA = pltpu.SemaphoreType.DMA
-ROWS = UPDATES * CELLROWS
 
 
 def gather_call(cells, weights, faces):
@@ -617,37 +706,22 @@
 def local(
     estimate, observed, psf_cells, tissue, neighbours, psf_list, psf_blend, cell_row, view_order
 ):
-    flags = jnp.concatenate([tissue, (neighbours[0] >= 0).astype(jnp.int32)])
-    est = jnp.pad(estimate.reshape(E, E, E), ((0, 0), (0, 0), (8, 72)))
-    views = view_order[:UPDATES]
-    lists = psf_list[0][views]
-    blend = psf_blend[0][views]
-    blend = blend / jnp.sum(blend, axis=1, keepdims=True)
-    number = jnp.arange(128, dtype=jnp.int32)
-    weights = jnp.sum(
-        jnp.where(lists[:, :, None] == number[None, None, :], blend[:, :, None], 0.0), axis=1
+    ints = jnp.concatenate([view_order, psf_list.reshape(12), tissue, neighbours.reshape(6)])
+    cp, weights, cells, faces = start_call(
+        ints, psf_blend.reshape(12), estimate.reshape(FLAT, 128), psf_cells.reshape(6, 1, KS3)
     )
-    weights = jnp.pad(weights, ((0, 8 - UPDATES), (0, 0)))
-    cells = jnp.concatenate(
-        [
-            lax.dynamic_index_in_dim(psf_cells[0], view_order[u], 0, keepdims=False)
-            for u in range(UPDATES)
-        ]
-    ).reshape(UPDATES, KS3)
-    cells = jnp.pad(cells, ((0, 0), (0, CELLROWS * 128 - KS3))).reshape(ROWS, 128)
-    seen = []
-    for update in range(UPDATES):
-        obs = lax.dynamic_index_in_dim(observed, view_order[update], 1, keepdims=False)
-        seen.append(jnp.pad(obs.reshape(E, E, E), ((0, 0), (0, 0), (8, 72))))
-    cp, *faces = start_call(est)
+    seen = [
+        lax.dynamic_index_in_dim(observed[0], view_order[u].astype(jnp.uint32), 0, keepdims=False).reshape(FLAT, 128)
+        for u in range(UPDATES)
+    ]
     gathered, shares, halos = gather_call(cells, weights, faces)
     kernel = collect_call(blend_call(cell_row, gathered, shares))
     taps = kernel.reshape(UPDATES, CELLROWS * 128)[:, :KS3].reshape(UPDATES, KS, KS, KS)
     taps = jnp.pad(taps, ((0, 0), (0, 0), (0, TAPROWS - KS), (0, 128 - KS)))
-    cp, *faces = update_call(False, flags, cp, seen[0], taps[0], halos)
+    cp, *faces = update_call(False, ints, cp, seen[0], taps[0], halos)
     halos = faces_call(faces)
-    result = update_call(True, flags, cp, seen[1], taps[1], halos)
-    return result[:, :, 8:56].reshape(1, E3)
+    result = update_call(True, ints, cp, seen[1], taps[1], halos)
+    return result.reshape(1, E3)
 
 
 def solution(mesh):

time: 106 us -> 91.4 us (0.86)
  local copies, waits for them, and re-layouts: 18.5 us -> 10.9 us
  between operations: 4.81 us -> 1.99 us
  other arithmetic: 3.66 us -> 1.33 us
  Pallas kernels: 78.8 us -> 76.6 us
    pad x5 -> x0, local copies, waits for them, and re-layouts: 4.13 us -> none  [the longest x2 2.09 us: local(): seen.append(jnp.pad(obs.reshape(E, E, E), ((0, 0), (0, 0), (8, 72))))]
    reshape x6 -> x2, local copies, waits for them, and re-layouts: 4.17 us -> 0.75 us  [the longest x1 0.67 us: local(): psf_blend.reshape(12)]
    unnamed x1 -> x0, other arithmetic: 2.71 us -> none
    dynamic_slice x2 -> x1, local copies, waits for them, and re-layouts: 3.43 us -> 5.41 us  [local(): lax.dynamic_index_in_dim(observed[0], view_order[u].astype(jnp.uint32), 0...]
    slice x2 -> x1, local copies, waits for them, and re-layouts: 3.03 us -> 1.34 us  [local(): view_order[u].astype(jnp.uint32)]
    pallas_call x1, Pallas kernels: 4.2 us -> 2.79 us  [start_call(): pl.pallas_call(start_kernel, out_shape=[jax.ShapeDtypeStruct((HALF, E, 12...]
    gather x2 -> x0, local copies, waits for them, and re-layouts: 1.12 us -> none  [the longest x1 0.56 us: local(): lists = psf_list[0][views]]
where the time goes in v2:
time: 91.4 us; the launch traced here: 90.9 us
  Pallas kernels  76.6 us (84%)
  local copies, waits for them, and re-layouts  10.9 us (12%)
  between operations  1.99 us (2%)
  other arithmetic  1.33 us (1%)
    pallas_call x2, Pallas kernels, update_call(): pl.pallas_call(functools.partial(update_kernel, last), out_shape=out_shap...  27.7 us
    pallas_call x1, Pallas kernels, gather_call(): pl.pallas_call(gather_kernel, out_shape=[jax.ShapeDtypeStruct((NEAR, ROWS...  18.9 us
    pallas_call x1, Pallas kernels, collect_call(): pl.pallas_call(collect_kernel, out_shape=jax.ShapeDtypeStruct((ROWS, 128)...  13.5 us
    pallas_call x1, Pallas kernels, faces_call(): pl.pallas_call(faces_kernel, out_shape=HALO_SHAPES, in_specs=[VMEM] * 6,...  10.2 us
    dynamic_slice x1, local copies, waits for them, and re-layouts, local(): lax.dynamic_index_in_dim(observed[0], view_order[u].astype(jnp.uint32), 0...  5.41 us
    pallas_call x1, Pallas kernels, blend_call(): pl.pallas_call(blend_kernel, out_shape=jax.ShapeDtypeStruct((FAR, ROWS, 1...  3.56 us
    pallas_call x1, Pallas kernels, start_call(): pl.pallas_call(start_kernel, out_shape=[jax.ShapeDtypeStruct((HALF, E, 12...  2.79 us

profile of v2, /device:TPU:0, one launch (start us, length us, event | category | flops | bytes accessed | tf_op | source)
XLA Modules:
  0.0 90.9 jit_solution(15297554490170711404)
XLA Ops:
  0.7 1.3 %fusion.2 = (s32[1]{0:T(128)}, s32[1]{0:T(128)}) fusion(s32[6]{0:T(128)} %param.27), kind=kLoop, calls=%fused_computation.7 | loop fusion | bytes 16 | tf_op jit(solution)/shard_map/slice | solution.py:714
  3.3 0.8 copy.22
  4.0 0.1 reshape.41
  4.1 1.3 %pad_add_fusion.ints_ref.flags_ref = s32[25]{0:T(128)} fusion(s32[6]{0:T(128)} %bitcast.18, s32[1]{0:T(128)S(6)} %copy.24, s32[12]{0:T(128)S(1)} %reshape.41, s32[6]{0:T(128)} %param.27), kind=kLoop, calls=%fused_computation.6 | loop fusion | flops 75 | bytes 200 | tf_op jit(solution)/shard_map/concatenate | solution.py:709
  5.5 0.8 copy.23
  6.2 0.7 reshape.43.blend_ref
  6.9 5.4 %dynamic-slice_reduce_fusion = (bf16[110592]{0:T(1024)(128)(2,1)}, bf16[110592]{0:T(1024)(128)(2,1)}) fusion(bf16[1,6,110592]{2,1,0:T(8,128)(2,1)} %param.20, u32[]{:T(128)} %bitcast.6, u32[]{:T(128)} %bitcast.3), kind=kLoop, calls=%fused_computation.2 | loop fusion | bytes 884744 | tf_op jit(solution)/shard_map/jit(dynamic_index_in_dim)/dynamic_slice | solution.py:714
  12.3 2.8 %start.1 = (f32[24,48,128]{2,1,0:T(8,128)}, f32[8,128]{1,0:T(8,128)}, f32[80,128]{1,0:T(8,128)}, bf16[384,128]{1,0:T(8,128)(2,1)}, bf16[384,128]{1,0:T(8,128)(2,...) custom-call(s32[25]{0:T(128)} %pad_add_fusion.ints_ref.flags_ref, ...), custom_call_target="tpu_custom_call" | custom-call | tf_op jit(solution)/shard_map/start/pallas_call | solution.py:416
  15.1 18.9 %gather.1 = (f32[8,80,128]{2,1,0:T(8,128)}, f32[16,8,128]{2,1,0:T(8,128)}, bf16[384,128]{1,0:T(8,128)(2,1)}, bf16[384,128]{1,0:T(8,128)(2,1)}, bf16[192,128]{1,0...) custom-call(f32[80,128]{1,0:T(8,128)} %get-tuple-element.36.cells_ref, ...), custom_call_target="tpu_custom_call" | custom-call | tf_op jit(solution)/shard_map/gather/pallas_call | solution.py:647
  34.0 3.6 %blend.1.parts_ref = f32[16,80,128]{2,1,0:T(8,128)} custom-call(s32[1,128]{1,0:T(1,128)} %bitcast.17, f32[8,80,128]{2,1,0:T(8,128)} %get-tuple-element.44.cells_ref, f32[16,8,128]{2,1,0:T(8,128)} %get-tuple-element.45.weights_ref), custom_call_target="tpu_custom_call" | custom-call | tf_op jit(solution)/shard_map/blend/pallas_call | solution.py:672
  37.6 13.5 %collect.1 = f32[80,128]{1,0:T(8,128)} custom-call(f32[16,80,128]{2,1,0:T(8,128)} %blend.1.parts_ref), custom_call_target="tpu_custom_call" | custom-call | tf_op jit(solution)/shard_map/collect/pallas_call | solution.py:683
  51.1 0.8 reshape.48
  51.9 0.2 reshape.49
  52.2 0.9 fusion.1
  53.0 13.8 %update.1 = (f32[24,48,128]{2,1,0:T(8,128)}, bf16[384,128]{1,0:T(8,128)(2,1)}, bf16[384,128]{1,0:T(8,128)(2,1)}, bf16[192,128]{1,0:T(8,128)(2,1)}, bf16[192,128]...) custom-call(s32[25]{0:T(128)} %pad_add_fusion.ints_ref.flags_ref, ...), custom_call_target="tpu_custom_call" | custom-call | tf_op jit(solution)/shard_map/update/pallas_call | solution.py:457
  66.8 10.2 %faces.1 = (bf16[384,128]{1,0:T(8,128)(2,1)}, bf16[384,128]{1,0:T(8,128)(2,1)}, bf16[192,128]{1,0:T(8,128)(2,1)}, bf16[192,128]{1,0:T(8,128)(2,1)}, bf16[144,128]{1,0:T(8,128)(2,1)}, /*index=5*/bf16[144,128]{1,0:T(8,128)(2,1)}) custom-call(bf16[384,128]{1,0:T(8,128)(2,1)} %get-tuple-element.53.refs_0_, bf16[384,128]{1,0:T(8,128)(2,1)} %get-tuple-element.54.refs_1_, ...), custom_call_target="tpu_custom_call" | custom-call | tf_op jit(solution)/shard_map/faces/pallas_call | solution.py:695
  77.0 13.9 %update_last.1 = f32[864,128]{1,0:T(8,128)} custom-call(s32[25]{0:T(128)} %pad_add_fusion.ints_ref.flags_ref, f32[24,48,128]{2,1,0:T(8,128)} %get-tuple-element.52.cp_ref, bf16[864,128]{1,0:T(8,128)(2,1)} %bitcast.14, f32[17,32,128]{2,1,0:T(8,128)} %get-tuple-element.67.taps_ref, bf16[384,128]{1,0:T(8,128)(2,1)} %get-tuple-element.59.hxm_ref, ...), custom_call_target="tpu_custom_call" | custom-call | tf_op jit(solution)/shard_map/update_last/pallas_call | solution.py:457
  (1 shorter events, 0.0 us)

commit v3 on v2

v3 whole, which is shorter than its diff:
```python
import functools
import math

import jax
import jax.numpy as jnp
import numpy as np
from jax import lax
from jax.experimental import pallas as pl
from jax.experimental.pallas import tpu as pltpu
from jax.sharding import PartitionSpec as P

E = 48
MARGIN = 8
UPDATES = 2
PAD = 64
KS = 17
E3 = 110592
KS3 = 4913
HALF = 24
PLANES = 40
TAPROWS = 32

CELLROWS = 40
ROWS = UPDATES * CELLROWS

F32 = jnp.float32
BF16 = jnp.bfloat16


def split_np(table):
    hi = np.asarray(table, np.float32).astype(jnp.bfloat16)
    lo = (np.asarray(table, np.float64) - hi.astype(np.float64)).astype(np.float32).astype(jnp.bfloat16)
    return hi, lo


def lane_table(table):
    hi, lo = split_np(table)
    row = np.concatenate([hi, lo], axis=1)
    return np.concatenate([row, row], axis=0)


def row_table(table):
    hi, lo = split_np(table)
    return np.concatenate([hi, hi, lo, lo], axis=1)


def make_tables():
    step = 2.0 * math.pi / PAD
    k = np.arange(PAD)
    ang = (k[:, None] * k[None, :] % PAD) * step
    cos, sin = np.cos(ang), np.sin(ang)
    fwd_z = np.block([[cos, -sin], [sin, cos]])
    inv_z = np.block([[cos, sin], [-sin, cos]]) / PAD
    fwd_y = np.concatenate([cos, sin], axis=0)
    inv_y = np.concatenate([cos[MARGIN : MARGIN + E], sin[MARGIN : MARGIN + E]], axis=0) / PAD
    t = np.arange(KS) - MARGIN
    ang_t = (t[:, None] * k[None, :]) % PAD * step
    tap_z = np.zeros((128, 128))
    tap_z[:KS, :PAD] = np.cos(ang_t)
    tap_z[:KS, PAD:] = -np.sin(ang_t)
    tap_y = np.zeros((128, TAPROWS))
    tap_y[:PAD, :KS] = np.cos(ang_t).T
    tap_y[PAD:, :KS] = np.sin(ang_t).T
    pack = np.zeros((2, 8 * 128, 128), np.float32)
    place = np.zeros((2, 128, 8 * 128), np.float32)
    for p in range(8):
        for s in range(2):
            for z in range(MARGIN):
                slot = p * 16 + s * 8 + z
                pack[0, p * 128 + s * 64 + MARGIN + z, slot] = 1
                pack[1, p * 128 + s * 64 + E + z, slot] = 1
                place[0, slot, p * 128 + s * 64 + z] = 1
                place[1, slot, p * 128 + s * 64 + MARGIN + E + z] = 1
    return dict(
        fwd_z=lane_table(fwd_z),
        inv_z=lane_table(inv_z),
        tap_z=lane_table(tap_z),
        fwd_y=row_table(fwd_y),
        inv_y=row_table(inv_y),
        tap_y=row_table(tap_y),
        pack=pack.astype(jnp.bfloat16),
        place=place.astype(jnp.bfloat16),
    )


TABLES = make_tables()


def split(values):
    hi = values.astype(BF16)
    lo = (values - hi.astype(F32)).astype(BF16)
    return hi, lo


def low_lanes(shape):
    return lax.broadcasted_iota(jnp.int32, shape, len(shape) - 1) < 64


def lane_sign(shape):
    return jnp.where(low_lanes(shape), 1.0, -1.0).astype(F32)


def dot(a, b):
    return lax.dot_general(a, b, (((1,), (0,)), ((), ())), preferred_element_type=F32)


def lanes_dft(rows, table):
    hi, lo = split(rows)
    both = dot(jnp.concatenate([hi, lo], axis=1), table)
    return both[:, :128] + both[:, 128:]


def rows_dft(planes, table, count, inverse):
    sign = lane_sign((count, 128))
    if inverse:
        sign = -sign
    out = []
    for a in range(0, len(planes), 2):
        cols = []
        for plane in planes[a : a + 2]:
            hi, lo = split(plane)
            cols.append(jnp.concatenate([hi, lo, hi, lo], axis=0))
        rhs = jnp.concatenate(cols, axis=1) if len(cols) > 1 else cols[0]
        both = dot(table, rhs)
        for b in range(len(cols)):
            c_part = both[:count, b * 128 : (b + 1) * 128]
            s_part = both[count : 2 * count, b * 128 : (b + 1) * 128]
            out.append(c_part + sign * pltpu.roll(s_part, 64, 1))
    return out


def emit_faces(cp_ref, pack_ref, faces):
    xm_ref, xp_ref, ym_ref, yp_ref, zm_ref, zp_ref = faces
    low = low_lanes((E, 128))
    for j in range(4):
        near = jnp.where(low, cp_ref[j], pltpu.roll(cp_ref[4 + j], 64, 1))
        xm_ref[j * E : (j + 1) * E, :] = near.astype(BF16)
        near = jnp.where(low, pltpu.roll(cp_ref[16 + j], 64, 1), cp_ref[20 + j])
        xp_ref[j * E : (j + 1) * E, :] = near.astype(BF16)
    ym_ref[...] = cp_ref[:, 0:8, :].reshape(HALF * 8, 128).astype(BF16)
    yp_ref[...] = cp_ref[:, E - 8 : E, :].reshape(HALF * 8, 128).astype(BF16)
    for g in range(3):
        wide = jnp.concatenate([cp_ref[g * 8 + p].astype(BF16) for p in range(8)], axis=1)
        zm_ref[g * E : (g + 1) * E, :] = dot(wide, pack_ref[0]).astype(BF16)
        zp_ref[g * E : (g + 1) * E, :] = dot(wide, pack_ref[1]).astype(BF16)


FACE_SHAPES = [(4 * E, 128), (4 * E, 128), (HALF * 8, 128), (HALF * 8, 128), (3 * E, 128), (3 * E, 128)]


def flat_to_pairs(load, store):
    for j in range(8):
        total = None
        for half in range(2):
            first = 48 * j
            k, lane = first // 128, first % 128
            base = MARGIN + 64 * half
            value = load(k, half)
            part = value if lane == base else pltpu.roll(value, (base - lane) % 128, 1)
            at = lax.broadcasted_iota(jnp.int32, part.shape, 1) - base
            length = min(48, 128 - lane)
            picked = jnp.where((at >= 0) & (at < length), part, 0.0)
            if length < 48:
                more = pltpu.roll(load(k + 1, half), base + length, 1)
                picked = jnp.where((at >= length) & (at < 48), more, picked)
            total = picked if total is None else total + picked
        store(j, total)


def pairs_to_flat(load, store):
    for half in range(2):
        for k in range(3):
            total = None
            for j in range(8):
                lane = 48 * j - 128 * k
                if lane <= -48 or lane >= 128:
                    continue
                value = pltpu.roll(load(j), (lane - MARGIN - 64 * half) % 128, 1)
                at = lax.broadcasted_iota(jnp.int32, value.shape, 1) - lane
                picked = jnp.where((at >= 0) & (at < 48), value, 0.0)
                total = picked if total is None else total + picked
            store(k, half, total)


GROUPS = HALF * E // 8
FLAT = E3 // 128


def load_flat(ref):
    return lambda k, half: ref[pl.ds(half * 3 * GROUPS + k, GROUPS, stride=3), :]


def store_rows(ref):
    def store(j, rows):
        ref[pl.ds(j, GROUPS, stride=8), :] = rows

    return store


def prepare(ints_ref, blend_ref, est_ref, cells_ref, pack_ref, cp_ref, weights_ref, own_ref, faces, flat_ref):
    number = lax.broadcasted_iota(jnp.int32, (1, 128), 1)
    weights_ref[...] = jnp.zeros_like(weights_ref)
    own_ref[...] = jnp.zeros_like(own_ref)
    for u in range(UPDATES):
        view = ints_ref[u]
        first = jnp.full((1, 128), blend_ref[2 * view], F32)
        second = jnp.full((1, 128), blend_ref[2 * view + 1], F32)
        total = first + second
        weights_ref[u : u + 1, :] = jnp.where(number == ints_ref[6 + 2 * view], first / total, 0.0) + jnp.where(
            number == ints_ref[7 + 2 * view], second / total, 0.0
        )
        for i in range(KS3 // 128):
            own_ref[u, i : i + 1, :] = cells_ref[view, :, i * 128 : (i + 1) * 128]
        tail = KS3 // 128 * 128
        i = KS3 // 128
        own_ref[u, i : i + 1, 0 : KS3 - tail] = cells_ref[view, :, tail:KS3]
    flat_to_pairs(load_flat(est_ref), store_rows(flat_ref))
    cp_ref[...] = flat_ref[...].reshape(HALF, E, 128)
    emit_faces(cp_ref, pack_ref, faces)


def forward_planes(src_ref, z_ref, spec_ref, rows, fwd_z_ref, fwd_y_ref):
    group = 20

    def z_body(it, carry):
        block = src_ref[pl.ds(it * group, group)].reshape(group * rows, 128)
        z_ref[pl.ds(it * group, group), 0:rows, :] = lanes_dft(block, fwd_z_ref[...]).reshape(group, rows, 128)
        return carry

    lax.fori_loop(0, PLANES // group, z_body, 0)

    def y_body(it, carry):
        planes = [z_ref[it * group + j, 0:rows, :] for j in range(group)]
        for j, plane in enumerate(rows_dft(planes, fwd_y_ref[...], PAD, False)):
            spec_ref[it * group + j] = plane
        return carry

    lax.fori_loop(0, PLANES // group, y_body, 0)


def filter_planes(spec_ref, kr_ref, ki_ref, out_ref, conjugate):
    group = 12
    sign = lane_sign((8, 128))
    if not conjugate:
        sign = -sign

    def body(kb, carry):
        rows = pl.ds(pl.multiple_of(kb * 8, 8), 8)
        for first in range(0, HALF, group):
            values = {}
            acc_r, acc_i = [None] * group, [None] * group
            for d in range(KS):
                tap = d if conjugate else KS - 1 - d
                kr = kr_ref[tap, rows, :]
                ki = ki_ref[tap, rows, :]
                for j in range(group):
                    m = first + j + d
                    if m not in values:
                        values[m] = spec_ref[m, rows, :]
                    if d == 0:
                        acc_r[j] = kr * values[m]
                        acc_i[j] = ki * values[m]
                    else:
                        acc_r[j] = acc_r[j] + kr * values[m]
                        acc_i[j] = acc_i[j] + ki * values[m]
            for j in range(group):
                out_ref[first + j, rows, :] = acc_r[j] + sign * pltpu.roll(acc_i[j], 64, 1)
        return carry

    lax.fori_loop(0, PAD // 8, body, 0)


def inverse_planes(spec_ref, y_ref, out_ref, inv_y_ref, inv_z_ref):
    group = 12

    def y_body(it, carry):
        planes = [spec_ref[it * group + j] for j in range(group)]
        for j, plane in enumerate(rows_dft(planes, inv_y_ref[...], E, True)):
            y_ref[it * group + j, 0:E, :] = plane
        return carry

    lax.fori_loop(0, HALF // group, y_body, 0)

    def z_body(it, carry):
        block = y_ref[pl.ds(it * group, group), 0:E, :].reshape(group * E, 128)
        out_ref[pl.ds(it * group, group)] = lanes_dft(block, inv_z_ref[...]).reshape(group, E, 128)
        return carry

    lax.fori_loop(0, HALF // group, z_body, 0)


def tap_spectra(flat_ref, taps_ref, z_ref, kr_ref, ki_ref, tap_z_ref, tap_y_ref):
    lane = lax.broadcasted_iota(jnp.int32, (1, 128), 1)
    for r in range(KS * KS):
        i, at = KS * r // 128, KS * r % 128
        run = pltpu.roll(flat_ref[i : i + 1, :], (-at) % 128, 1)
        if at + KS > 128:
            more = pltpu.roll(flat_ref[i + 1 : i + 2, :], (-at) % 128, 1)
            run = jnp.where(lane < 128 - at, run, more)
        taps_ref[r // KS, r % KS : r % KS + 1, :] = run
    low_full = low_lanes((PAD, 128))
    rows = lanes_dft(taps_ref[...].reshape(KS * TAPROWS, 128), tap_z_ref[...])
    z_ref[0:KS, 0:TAPROWS, :] = rows.reshape(KS, TAPROWS, 128)
    planes = [z_ref[d, 0:TAPROWS, :] for d in range(KS)]
    for d, spec in enumerate(rows_dft(planes, tap_y_ref[...], PAD, False)):
        other = pltpu.roll(spec, 64, 1)
        kr_ref[d] = jnp.where(low_full, spec, other)
        ki_ref[d] = jnp.where(low_full, other, spec)


def assemble(ints_ref, cp_ref, halos, place_ref, ext_ref, pp_ref):
    hxm_ref, hxp_ref, hym_ref, hyp_ref, hzm_ref, hzp_ref = halos
    low_core = low_lanes((E, 128))
    low_row = low_lanes((8, 128))

    def face(ref, f):
        return jnp.where(ints_ref[19 + f] >= 0, ref[...].astype(F32), 0.0)

    ext_ref[:, 0:8, :] = face(hym_ref, 2).reshape(HALF, 8, 128)
    ext_ref[:, 56:64, :] = face(hyp_ref, 3).reshape(HALF, 8, 128)
    zm_all = face(hzm_ref, 4).astype(BF16)
    zp_all = face(hzp_ref, 5).astype(BF16)
    for g in range(3):
        zm = dot(zm_all[g * E : (g + 1) * E], place_ref[0])
        zp = dot(zp_all[g * E : (g + 1) * E], place_ref[1])
        for p in range(8):
            lanes = slice(p * 128, (p + 1) * 128)
            ext_ref[g * 8 + p, 8:56, :] = cp_ref[g * 8 + p] + zm[:, lanes] + zp[:, lanes]
    xm = face(hxm_ref, 0).reshape(4, E, 128)
    xp = face(hxp_ref, 1).reshape(4, E, 128)
    pp_ref[8:32] = ext_ref[...]
    for j in range(8):
        for rows in (slice(0, 8), slice(56, 64)):
            near = ext_ref[16 + j, rows, :]
            pp_ref[j, rows, :] = pltpu.roll(jnp.where(low_row, near, 0.0), 64, 1)
            near = ext_ref[j, rows, :]
            pp_ref[32 + j, rows, :] = pltpu.roll(jnp.where(low_row, 0.0, near), 64, 1)
        before = xm[j] if j < 4 else pltpu.roll(xm[j - 4], 64, 1)
        after = pltpu.roll(xp[j], 64, 1) if j < 4 else xp[j - 4]
        pp_ref[j, 8:56, :] = jnp.where(low_core, before, pltpu.roll(ext_ref[16 + j, 8:56, :], 64, 1))
        pp_ref[32 + j, 8:56, :] = jnp.where(low_core, pltpu.roll(ext_ref[j, 8:56, :], 64, 1), after)


def correct(ints_ref, cp_ref, new_ref, seen_ref, tables, work):
    fwd_z_ref, inv_z_ref, fwd_yc_ref, inv_y_ref = tables
    z_ref, spec_ref, kr_ref, ki_ref, fil_ref, core_ref, q_ref = work
    low_core = low_lanes((E, 128))
    filter_planes(spec_ref, kr_ref, ki_ref, fil_ref, False)
    inverse_planes(fil_ref, z_ref, core_ref, inv_y_ref, inv_z_ref)

    lane = lax.broadcasted_iota(jnp.int32, (E, 128), 1) % 64
    inside = (lane >= MARGIN) & (lane < MARGIN + E)

    def ratio_body(it, carry):
        for o in [it * 4 + j for j in range(4)]:
            q_ref[o + 8] = jnp.where(inside, seen_ref[o] / jnp.where(inside, core_ref[o], 1.0), 0.0)
        return carry

    lax.fori_loop(0, HALF // 4, ratio_body, 0)
    for j in range(8):
        q_ref[j] = pltpu.roll(jnp.where(low_core, q_ref[24 + j], 0.0), 64, 1)
        q_ref[32 + j] = pltpu.roll(jnp.where(low_core, 0.0, q_ref[8 + j]), 64, 1)

    forward_planes(q_ref, z_ref, spec_ref, E, fwd_z_ref, fwd_yc_ref)
    filter_planes(spec_ref, kr_ref, ki_ref, fil_ref, True)
    inverse_planes(fil_ref, z_ref, core_ref, inv_y_ref, inv_z_ref)

    alive = ints_ref[18] > 0

    def finish(it, carry):
        for o in [it * 4 + j for j in range(4)]:
            old = cp_ref[o]
            new_ref[o] = jnp.where(jnp.logical_and(inside, alive), old * core_ref[o], old)
        return carry

    lax.fori_loop(0, HALF // 4, finish, 0)


VMEM = pl.BlockSpec(memory_space=pltpu.VMEM)
SMEM = pl.BlockSpec(memory_space=pltpu.SMEM)


def fwd_y_core():
    full = TABLES["fwd_y"]
    return np.concatenate([full[:, s * PAD + MARGIN : s * PAD + MARGIN + E] for s in range(4)], axis=1)


GRID = (4, 4, 8)


def coords_of(b):
    return (
        b % 2 + 2 * ((b // 8) % 2),
        (b // 2) % 2 + 2 * ((b // 16) % 2),
        (b // 64) % 2 + 2 * ((b // 4) % 2) + 4 * ((b // 32) % 2),
    )


def block_at(c):
    return (
        c[0] % 2 + 2 * (c[1] % 2) + 4 * ((c[2] // 2) % 2) + 8 * (c[0] // 2) + 16 * (c[1] // 2)
        + 32 * (c[2] // 4) + 64 * (c[2] % 2)
    )


def neighbour_of(b, axis, step):
    c = list(coords_of(b))
    c[axis] = (c[axis] + step + GRID[axis]) % GRID[axis]
    return block_at(c)


MESH = pl.DeviceIdType.MESH
NEAR = 8
FAR = 16


def near_peers(me):
    base = me // NEAR * NEAR
    return [base + (me % NEAR + s) % NEAR for s in range(1, NEAR)]


def far_peers(me):
    return [(me // NEAR + s) % FAR * NEAR + me % NEAR for s in range(1, FAR)]


def face_peers(me):
    return [neighbour_of(me, f // 2, -1 if f % 2 == 0 else 1) for f in range(6)]


def face_copies(faces, halos, peers, send, recv):
    return [
        pltpu.make_async_remote_copy(
            src_ref=faces[f],
            dst_ref=halos[f ^ 1],
            send_sem=send.at[f],
            recv_sem=recv.at[f],
            device_id=(peers[f],),
            device_id_type=MESH,
        )
        for f in range(6)
    ]


def remote(src, dst, send, recv, peer):
    return pltpu.make_async_remote_copy(
        src_ref=src, dst_ref=dst, send_sem=send, recv_sem=recv, device_id=(peer,), device_id_type=MESH
    )


def blend_cells(u, cells_ref, weights_ref, pick, scaled_ref, parts_ref):
    for a in range(NEAR):
        cell = cells_ref[a]
        total = jnp.sum(jnp.sum(cell, axis=0, keepdims=True), axis=1, keepdims=True)
        scaled_ref[a] = cell / total

    def body(dest, carry):
        share = jnp.sum(weights_ref[dest, u : u + 1, :] * pick, axis=1, keepdims=True)
        total = share[0:1, :] * scaled_ref[0]
        for a in range(1, NEAR):
            total = total + share[a : a + 1, :] * scaled_ref[a]
        parts_ref[dest] = total
        return carry

    lax.fori_loop(0, FAR, body, 0)


def whole_kernel(*refs):
    ints_ref, blend_ref, est_ref, cells_ref, cell_row_ref = refs[:5]
    seen_in = refs[5:7]
    fwd_z_ref, inv_z_ref, tap_z_ref, fwd_y_ref, fwd_yc_ref, inv_y_ref, tap_y_ref, pack_ref, place_ref = refs[7:16]
    out_ref = refs[16]
    refs = refs[17:]
    cp_refs, own_ref, weights_ref = refs[:2], refs[2], refs[3]
    faces = (refs[4:10], refs[10:16])
    halos = (refs[16:22], refs[22:28])
    near_all, weights_all, parts, held = refs[28:30], refs[30], refs[31:33], refs[33:35]
    scaled_ref, kernel_ref, taps_ref, ext_ref, pp_ref, z_ref, spec_ref = refs[35:42]
    kr_ref, ki_ref, fil_ref, core_ref, q_ref, wide_ref, flat_ref = refs[42:49]
    own_sem, near_send, near_recv, share_send, share_recv = refs[49:54]
    far_send, far_recv, face_send, face_recv = refs[54:58]
    row_ref = flat_ref.reshape(HALF * E, 128)
    tables = (fwd_z_ref, inv_z_ref, fwd_yc_ref, inv_y_ref)
    work = (z_ref, spec_ref, kr_ref, ki_ref, fil_ref, core_ref, q_ref)

    me = lax.axis_index("blk")
    near, far, across = near_peers(me), far_peers(me), face_peers(me)
    barrier = pltpu.get_barrier_semaphore()
    for peer in near + far + across:
        pl.semaphore_signal(barrier, inc=1, device_id=(peer,), device_id_type=MESH)

    taps_ref[...] = jnp.zeros_like(taps_ref)
    prepare(
        ints_ref, blend_ref, est_ref, cells_ref, pack_ref, cp_refs[0], weights_ref, own_ref, faces[0], row_ref
    )
    pl.semaphore_wait(barrier, len(near + far + across))

    near_copies = [
        [
            remote(own_ref.at[u], near_all[u].at[me % NEAR], near_send.at[u, s], near_recv.at[u, s], peer)
            for s, peer in enumerate(near)
        ]
        + [pltpu.make_async_copy(own_ref.at[u], near_all[u].at[me % NEAR], own_sem.at[u])]
        for u in range(UPDATES)
    ]
    share_copies = [
        remote(weights_ref, weights_all.at[me // NEAR], share_send.at[s], share_recv.at[s], peer)
        for s, peer in enumerate(far)
    ] + [pltpu.make_async_copy(weights_ref, weights_all.at[me // NEAR], own_sem.at[2])]
    face_copies = [
        [
            remote(faces[u][f], halos[u][f ^ 1], face_send.at[u, f], face_recv.at[u, f], across[f])
            for f in range(6)
        ]
        for u in range(UPDATES)
    ]
    far_copies = [
        [
            remote(parts[u].at[(me // NEAR + 1 + s) % FAR], held[u].at[s], far_send.at[u, s], far_recv.at[u, s], peer)
            for s, peer in enumerate(far)
        ]
        for u in range(UPDATES)
    ]

    def start(copies):
        for copy in copies:
            copy.start()

    def wait(copies):
        for copy in copies:
            copy.wait()

    base = me // NEAR * NEAR
    pick = (cell_row_ref[...] == base + lax.broadcasted_iota(jnp.int32, (NEAR, 128), 0)).astype(F32)

    def seen_pairs(u):
        wide_ref[...] = seen_in[u][...].astype(F32)
        flat_to_pairs(load_flat(wide_ref), store_rows(row_ref))

    def spectra(u):
        wait(far_copies[u])
        total = parts[u][me // NEAR]
        for s in range(FAR - 1):
            total = total + held[u][s]
        kernel_ref[...] = total
        tap_spectra(kernel_ref, taps_ref, z_ref, kr_ref, ki_ref, tap_z_ref, tap_y_ref)

    def padded_spectra(u):
        wait(face_copies[u])
        assemble(ints_ref, cp_refs[u], halos[u], place_ref, ext_ref, pp_ref)
        forward_planes(pp_ref, z_ref, spec_ref, PAD, fwd_z_ref, fwd_y_ref)

    start(near_copies[0])
    start(share_copies)
    start(face_copies[0])
    start(near_copies[1])
    seen_pairs(0)
    wait(near_copies[0])
    wait(share_copies)
    blend_cells(0, near_all[0], weights_all, pick, scaled_ref, parts[0])
    start(far_copies[0])
    padded_spectra(0)
    wait(near_copies[1])
    blend_cells(1, near_all[1], weights_all, pick, scaled_ref, parts[1])
    start(far_copies[1])
    spectra(0)
    correct(ints_ref, cp_refs[0], cp_refs[1], flat_ref, tables, work)
    emit_faces(cp_refs[1], pack_ref, faces[1])
    start(face_copies[1])
    spectra(1)
    seen_pairs(1)
    padded_spectra(1)
    correct(ints_ref, cp_refs[1], flat_ref, flat_ref, tables, work)

    def load_new(j):
        return row_ref[pl.ds(j, GROUPS, stride=8), :]

    def store_new(k, half, rows):
        out_ref[pl.ds(half * 3 * GROUPS + k, GROUPS, stride=3), :] = rows

    pairs_to_flat(load_new, store_new)


HALO_SHAPES = [FACE_SHAPES[f ^ 1] for f in range(6)]
DMA = pltpu.SemaphoreType.DMA


def whole_call(ints, blend, est, cells, cell_row, seen):
    tables = [
        TABLES["fwd_z"],
        TABLES["inv_z"],
        TABLES["tap_z"],
        TABLES["fwd_y"],
        fwd_y_core(),
        TABLES["inv_y"],
        TABLES["tap_y"],
        TABLES["pack"],
        TABLES["place"],
    ]
    f32 = [
        (NEAR, CELLROWS, 128),
        (NEAR, CELLROWS, 128),
        (FAR, 8, 128),
        (FAR, CELLROWS, 128),
        (FAR, CELLROWS, 128),
        (FAR - 1, CELLROWS, 128),
        (FAR - 1, CELLROWS, 128),
        (NEAR, CELLROWS, 128),
        (CELLROWS, 128),
        (KS, TAPROWS, 128),
        (HALF, PAD, 128),
        (PLANES, PAD, 128),
        (PLANES, PAD, 128),
        (PLANES, PAD, 128),
        (KS, PAD, 128),
        (KS, PAD, 128),
        (HALF, PAD, 128),
        (HALF, E, 128),
        (PLANES, E, 128),
        (FLAT, 128),
        (HALF, E, 128),
    ]
    scratch = [pltpu.VMEM(s, F32) for s in [(HALF, E, 128)] * 2 + [(UPDATES, CELLROWS, 128), (8, 128)]]
    scratch += [pltpu.VMEM(s, BF16) for s in FACE_SHAPES * 2 + HALO_SHAPES * 2]
    scratch += [pltpu.VMEM(s, F32) for s in f32]
    scratch += [DMA((3,)), DMA((2, NEAR - 1)), DMA((2, NEAR - 1)), DMA((FAR - 1,)), DMA((FAR - 1,))]
    scratch += [DMA((2, FAR - 1)), DMA((2, FAR - 1)), DMA((2, 6)), DMA((2, 6))]
    return pl.pallas_call(
        whole_kernel,
        out_shape=jax.ShapeDtypeStruct((FLAT, 128), F32),
        in_specs=[SMEM] * 2 + [VMEM] * (5 + len(tables)),
        out_specs=VMEM,
        scratch_shapes=scratch,
        compiler_params=pltpu.CompilerParams(collective_id=0, has_side_effects=True),
        name="whole",
    )(ints, blend, est, cells, cell_row.reshape(1, 128), *seen, *[jnp.asarray(t) for t in tables])


def local(
    estimate, observed, psf_cells, tissue, neighbours, psf_list, psf_blend, cell_row, view_order
):
    ints = jnp.concatenate([view_order, psf_list.reshape(12), tissue, neighbours.reshape(6)])
    seen = [
        lax.dynamic_index_in_dim(observed[0], view_order[u].astype(jnp.uint32), 0, keepdims=False).reshape(FLAT, 128)
        for u in range(UPDATES)
    ]
    result = whole_call(
        ints, psf_blend.reshape(12), estimate.reshape(FLAT, 128), psf_cells.reshape(6, 1, KS3), cell_row, seen
    )
    return result.reshape(1, E3)


def solution(mesh):
    return jax.shard_map(
        local,
        mesh=mesh,
        in_specs=(
            P("blk", None),
            P("blk", None, None),
            P("blk", None, None),
            P("blk"),
            P("blk", None),
            P("blk", None, None),
            P("blk", None, None),
            P(),
            P(),
        ),
        out_specs=P("blk", None),
        check_vma=False,
    )
```

time: 91.4 us -> 64.5 us (0.71)
  Pallas kernels: 76.6 us -> 50.2 us
    pallas_call x7 -> x1, Pallas kernels: 76.6 us -> 50.2 us  [whole_call(): pl.pallas_call(whole_kernel, out_shape=jax.ShapeDtypeStruct((FLAT, 128),...]
    unnamed x2 -> x3, local copies, waits for them, and re-layouts: 1.53 us -> 3.34 us
    reshape x2 -> x0, local copies, waits for them, and re-layouts: 1.03 us -> none  [local(): kernel.reshape(UPDATES, CELLROWS * 128)[:, :KS3]]
where the time goes in v3:
time: 64.5 us; the launch traced here: 64.3 us
  Pallas kernels  50.2 us (78%)
  local copies, waits for them, and re-layouts  10.9 us (17%)
  between operations  1.88 us (3%)
  other arithmetic  1.32 us (2%)
    pallas_call x1, Pallas kernels, whole_call(): pl.pallas_call(whole_kernel, out_shape=jax.ShapeDtypeStruct((FLAT, 128),...  50.2 us
    dynamic_slice x1, local copies, waits for them, and re-layouts, local(): lax.dynamic_index_in_dim(observed[0], view_order[u].astype(jnp.uint32), 0...  5.52 us
    unnamed x3, local copies, waits for them, and re-layouts  3.34 us
    concatenate x1, other arithmetic, local(): jnp.concatenate([view_order, psf_list.reshape(12), tissue, neighbours.res...  1.32 us
    slice x1, local copies, waits for them, and re-layouts, local(): view_order[u].astype(jnp.uint32)  1.31 us

profile of v3, /device:TPU:0, one launch (start us, length us, event | category | flops | bytes accessed | tf_op | source)
XLA Modules:
  0.0 64.3 jit_solution(5599255218917954919)
XLA Ops:
  0.7 1.3 %fusion = (s32[1]{0:T(128)}, s32[1]{0:T(128)}) fusion(s32[6]{0:T(128)} %param.26), kind=kLoop, calls=%fused_computation.3 | loop fusion | bytes 16 | tf_op jit(solution)/shard_map/slice | solution.py:643
  3.2 0.8 %copy.21 = s32[1,6,2]{2,1,0:T(8,128)S(1)} copy(s32[1,6,2]{1,2,0:T(2,128)} %param.23) | data formatting | bytes 96 | tf_op args[5]
  3.9 0.1 reshape.35
  4.0 1.3 %pad_add_fusion.refs_0_ = s32[25]{0:T(128)} fusion(s32[6]{0:T(128)} %bitcast.15, s32[1]{0:T(128)S(6)} %copy.24, s32[12]{0:T(128)S(1)} %reshape.35, s32[6]{0:T(128)} %param.26), kind=kLoop, calls=%fused_computation.2 | loop fusion | flops 75 | bytes 200 | tf_op jit(solution)/shard_map/concatenate | solution.py:641
  5.3 0.8 %copy.22 = f32[1,6,2]{2,1,0:T(8,128)S(1)} copy(f32[1,6,2]{1,2,0:T(2,128)} %param.24) | data formatting | bytes 96 | tf_op args[6]
  6.1 0.6 reshape.37.refs_1_
  6.7 5.5 %dynamic-slice_reduce_fusion = (bf16[110592]{0:T(1024)(128)(2,1)}, bf16[110592]{0:T(1024)(128)(2,1)}) fusion(bf16[1,6,110592]{2,1,0:T(8,128)(2,1)} %param.19, u32[]{:T(128)} %bitcast.5, u32[]{:T(128)} %bitcast.4), kind=kLoop, calls=%fused_computation | loop fusion | bytes 884744 | tf_op jit(solution)/shard_map/jit(dynamic_index_in_dim)/dynamic_slice | solution.py:643
  12.2 50.2 %whole.1 = f32[864,128]{1,0:T(8,128)} custom-call(s32[25]{0:T(128)} %pad_add_fusion.refs_0_, f32[12]{0:T(128)} %reshape.37.refs_1_, f32[864,128]{1,0:T(8,128)} %bitcast.12, f32[6,1,4913]{2,1,0:T(1,128)} %bitcast.13, s32[1,128]{1,0:T(1,128)} %bitcast.14, bf16[864,128]{1,0:T(8,128)(2,1)} %bitcast.11, bf16[864,128]{1,0:T(8,128)(2,1)} %bitcast.10, ...), custom_call_target="tpu_custom_call" | custom-call | tf_op jit(solution)/shard_map/whole/pallas_call | solution.py:627
  62.4 1.8 %copy.25 = f32[1,110592]{1,0:T(1,128)} copy(f32[1,110592]{1,0:T(1,128)} %bitcast.9) | data formatting | bytes 884736

commit v4 on v3

--- a/solution.py
+++ b/solution.py
@@ -197,17 +197,17 @@
     return store
 
 
-def prepare(ints_ref, blend_ref, est_ref, cells_ref, pack_ref, cp_ref, weights_ref, own_ref, faces, flat_ref):
+def prepare(order_ref, list_ref, blend_ref, est_ref, cells_ref, pack_ref, cp_ref, weights_ref, own_ref, faces, flat_ref):
     number = lax.broadcasted_iota(jnp.int32, (1, 128), 1)
     weights_ref[...] = jnp.zeros_like(weights_ref)
     own_ref[...] = jnp.zeros_like(own_ref)
     for u in range(UPDATES):
-        view = ints_ref[u]
-        first = jnp.full((1, 128), blend_ref[2 * view], F32)
-        second = jnp.full((1, 128), blend_ref[2 * view + 1], F32)
+        view = order_ref[u]
+        first = jnp.full((1, 128), blend_ref[0, view], F32)
+        second = jnp.full((1, 128), blend_ref[1, view], F32)
         total = first + second
-        weights_ref[u : u + 1, :] = jnp.where(number == ints_ref[6 + 2 * view], first / total, 0.0) + jnp.where(
-            number == ints_ref[7 + 2 * view], second / total, 0.0
+        weights_ref[u : u + 1, :] = jnp.where(number == list_ref[0, view], first / total, 0.0) + jnp.where(
+            number == list_ref[1, view], second / total, 0.0
         )
         for i in range(KS3 // 128):
             own_ref[u, i : i + 1, :] = cells_ref[view, :, i * 128 : (i + 1) * 128]
@@ -308,13 +308,13 @@
         ki_ref[d] = jnp.where(low_full, other, spec)
 
 
-def assemble(ints_ref, cp_ref, halos, place_ref, ext_ref, pp_ref):
+def assemble(next_ref, cp_ref, halos, place_ref, ext_ref, pp_ref):
     hxm_ref, hxp_ref, hym_ref, hyp_ref, hzm_ref, hzp_ref = halos
     low_core = low_lanes((E, 128))
     low_row = low_lanes((8, 128))
 
     def face(ref, f):
-        return jnp.where(ints_ref[19 + f] >= 0, ref[...].astype(F32), 0.0)
+        return jnp.where(next_ref[0, f] >= 0, ref[...].astype(F32), 0.0)
 
     ext_ref[:, 0:8, :] = face(hym_ref, 2).reshape(HALF, 8, 128)
     ext_ref[:, 56:64, :] = face(hyp_ref, 3).reshape(HALF, 8, 128)
@@ -341,7 +341,7 @@
         pp_ref[32 + j, 8:56, :] = jnp.where(low_core, pltpu.roll(ext_ref[j, 8:56, :], 64, 1), after)
 
 
-def correct(ints_ref, cp_ref, new_ref, seen_ref, tables, work):
+def correct(tissue_ref, cp_ref, new_ref, seen_ref, tables, work):
     fwd_z_ref, inv_z_ref, fwd_yc_ref, inv_y_ref = tables
     z_ref, spec_ref, kr_ref, ki_ref, fil_ref, core_ref, q_ref = work
     low_core = low_lanes((E, 128))
@@ -365,7 +365,7 @@
     filter_planes(spec_ref, kr_ref, ki_ref, fil_ref, True)
     inverse_planes(fil_ref, z_ref, core_ref, inv_y_ref, inv_z_ref)
 
-    alive = ints_ref[18] > 0
+    alive = tissue_ref[0] > 0
 
     def finish(it, carry):
         for o in [it * 4 + j for j in range(4)]:
@@ -465,11 +465,17 @@
 
 
 def whole_kernel(*refs):
-    ints_ref, blend_ref, est_ref, cells_ref, cell_row_ref = refs[:5]
-    seen_in = refs[5:7]
-    fwd_z_ref, inv_z_ref, tap_z_ref, fwd_y_ref, fwd_yc_ref, inv_y_ref, tap_y_ref, pack_ref, place_ref = refs[7:16]
-    out_ref = refs[16]
-    refs = refs[17:]
+    order_ref, list_ref, blend_ref, tissue_ref, next_ref = refs[:5]
+    inputs = refs[5 : 5 + INPUTS]
+    out_ref = refs[5 + INPUTS]
+    local_refs = refs[6 + INPUTS : 6 + 2 * INPUTS]
+    load_sem = refs[6 + 2 * INPUTS]
+    refs = refs[7 + 2 * INPUTS :]
+    loads = [pltpu.make_async_copy(inputs[i], local_refs[i], load_sem.at[i]) for i in range(INPUTS)]
+    est_ref, cells_ref, cell_row_ref, pack_ref, seen_in, place_ref = local_refs[:6]
+    fwd_z_ref, fwd_y_ref, tap_z_ref, tap_y_ref, inv_y_ref, inv_z_ref, fwd_yc_ref = local_refs[6:]
+    for load in loads:
+        load.start()
     cp_refs, own_ref, weights_ref = refs[:2], refs[2], refs[3]
     faces = (refs[4:10], refs[10:16])
     halos = (refs[16:22], refs[22:28])
@@ -489,8 +495,20 @@
         pl.semaphore_signal(barrier, inc=1, device_id=(peer,), device_id_type=MESH)
 
     taps_ref[...] = jnp.zeros_like(taps_ref)
+    for load in loads[:4]:
+        load.wait()
     prepare(
-        ints_ref, blend_ref, est_ref, cells_ref, pack_ref, cp_refs[0], weights_ref, own_ref, faces[0], row_ref
+        order_ref,
+        list_ref,
+        blend_ref,
+        est_ref,
+        cells_ref,
+        pack_ref,
+        cp_refs[0],
+        weights_ref,
+        own_ref,
+        faces[0],
+        row_ref,
     )
     pl.semaphore_wait(barrier, len(near + far + across))
 
@@ -532,9 +550,19 @@
     base = me // NEAR * NEAR
     pick = (cell_row_ref[...] == base + lax.broadcasted_iota(jnp.int32, (NEAR, 128), 0)).astype(F32)
 
+    def widen(it, carry):
+        for j in range(8):
+            at = pl.multiple_of(it * 1024 + j * 128, 128)
+            wide_ref[pl.ds(pl.multiple_of(it * 64 + j * 8, 8), 6), :] = seen_in[:, pl.ds(at, 128)].astype(F32)
+        return carry
+
     def seen_pairs(u):
-        wide_ref[...] = seen_in[u][...].astype(F32)
-        flat_to_pairs(load_flat(wide_ref), store_rows(row_ref))
+        view = order_ref[u]
+
+        def load(k, half):
+            return wide_ref[pl.ds((half * 3 * GROUPS + k) * 8 + view, GROUPS, stride=24), :]
+
+        flat_to_pairs(load, store_rows(row_ref))
 
     def spectra(u):
         wait(far_copies[u])
@@ -546,13 +574,16 @@
 
     def padded_spectra(u):
         wait(face_copies[u])
-        assemble(ints_ref, cp_refs[u], halos[u], place_ref, ext_ref, pp_ref)
+        assemble(next_ref, cp_refs[u], halos[u], place_ref, ext_ref, pp_ref)
         forward_planes(pp_ref, z_ref, spec_ref, PAD, fwd_z_ref, fwd_y_ref)
 
     start(near_copies[0])
     start(share_copies)
     start(face_copies[0])
     start(near_copies[1])
+    for load in loads[4:]:
+        load.wait()
+    lax.fori_loop(0, FLAT // 8, widen, 0)
     seen_pairs(0)
     wait(near_copies[0])
     wait(share_copies)
@@ -563,13 +594,13 @@
     blend_cells(1, near_all[1], weights_all, pick, scaled_ref, parts[1])
     start(far_copies[1])
     spectra(0)
-    correct(ints_ref, cp_refs[0], cp_refs[1], flat_ref, tables, work)
+    correct(tissue_ref, cp_refs[0], cp_refs[1], flat_ref, tables, work)
     emit_faces(cp_refs[1], pack_ref, faces[1])
     start(face_copies[1])
     spectra(1)
     seen_pairs(1)
     padded_spectra(1)
-    correct(ints_ref, cp_refs[1], flat_ref, flat_ref, tables, work)
+    correct(tissue_ref, cp_refs[1], flat_ref, flat_ref, tables, work)
 
     def load_new(j):
         return row_ref[pl.ds(j, GROUPS, stride=8), :]
@@ -582,19 +613,24 @@
 
 HALO_SHAPES = [FACE_SHAPES[f ^ 1] for f in range(6)]
 DMA = pltpu.SemaphoreType.DMA
-
-
-def whole_call(ints, blend, est, cells, cell_row, seen):
-    tables = [
-        TABLES["fwd_z"],
-        TABLES["inv_z"],
-        TABLES["tap_z"],
-        TABLES["fwd_y"],
-        fwd_y_core(),
-        TABLES["inv_y"],
-        TABLES["tap_y"],
-        TABLES["pack"],
-        TABLES["place"],
+INPUTS = 13
+
+
+def whole_call(scalars, est, cells, cell_row, seen):
+    inputs = [
+        est,
+        cells,
+        cell_row,
+        jnp.asarray(TABLES["pack"]),
+        seen,
+        jnp.asarray(TABLES["place"]),
+        jnp.asarray(TABLES["fwd_z"]),
+        jnp.asarray(TABLES["fwd_y"]),
+        jnp.asarray(TABLES["tap_z"]),
+        jnp.asarray(TABLES["tap_y"]),
+        jnp.asarray(TABLES["inv_y"]),
+        jnp.asarray(TABLES["inv_z"]),
+        jnp.asarray(fwd_y_core()),
     ]
     f32 = [
         (NEAR, CELLROWS, 128),
@@ -616,10 +652,11 @@
         (HALF, PAD, 128),
         (HALF, E, 128),
         (PLANES, E, 128),
-        (FLAT, 128),
+        (FLAT * 8, 128),
         (HALF, E, 128),
     ]
-    scratch = [pltpu.VMEM(s, F32) for s in [(HALF, E, 128)] * 2 + [(UPDATES, CELLROWS, 128), (8, 128)]]
+    scratch = [pltpu.VMEM(x.shape, x.dtype) for x in inputs] + [DMA((INPUTS,))]
+    scratch += [pltpu.VMEM(s, F32) for s in [(HALF, E, 128)] * 2 + [(UPDATES, CELLROWS, 128), (8, 128)]]
     scratch += [pltpu.VMEM(s, BF16) for s in FACE_SHAPES * 2 + HALO_SHAPES * 2]
     scratch += [pltpu.VMEM(s, F32) for s in f32]
     scratch += [DMA((3,)), DMA((2, NEAR - 1)), DMA((2, NEAR - 1)), DMA((FAR - 1,)), DMA((FAR - 1,))]
@@ -627,24 +664,30 @@
     return pl.pallas_call(
         whole_kernel,
         out_shape=jax.ShapeDtypeStruct((FLAT, 128), F32),
-        in_specs=[SMEM] * 2 + [VMEM] * (5 + len(tables)),
+        in_specs=[SMEM] * 5 + [pl.BlockSpec(memory_space=pl.ANY)] * INPUTS,
         out_specs=VMEM,
         scratch_shapes=scratch,
         compiler_params=pltpu.CompilerParams(collective_id=0, has_side_effects=True),
         name="whole",
-    )(ints, blend, est, cells, cell_row.reshape(1, 128), *seen, *[jnp.asarray(t) for t in tables])
+    )(*scalars, *inputs)
 
 
 def local(
     estimate, observed, psf_cells, tissue, neighbours, psf_list, psf_blend, cell_row, view_order
 ):
-    ints = jnp.concatenate([view_order, psf_list.reshape(12), tissue, neighbours.reshape(6)])
-    seen = [
-        lax.dynamic_index_in_dim(observed[0], view_order[u].astype(jnp.uint32), 0, keepdims=False).reshape(FLAT, 128)
-        for u in range(UPDATES)
-    ]
+    scalars = (
+        view_order,
+        psf_list.transpose(0, 2, 1).reshape(2, 6),
+        psf_blend.transpose(0, 2, 1).reshape(2, 6),
+        tissue,
+        neighbours,
+    )
     result = whole_call(
-        ints, psf_blend.reshape(12), estimate.reshape(FLAT, 128), psf_cells.reshape(6, 1, KS3), cell_row, seen
+        scalars,
+        estimate.reshape(FLAT, 128),
+        psf_cells.reshape(6, 1, KS3),
+        cell_row.reshape(1, 128),
+        observed.reshape(6, E3),
     )
     return result.reshape(1, E3)
 

time: 64.5 us -> 51.9 us (0.80)
  local copies, waits for them, and re-layouts: 10.9 us -> 1.8 us
  other arithmetic: 1.32 us -> 0 us
  between operations: 1.88 us -> 0.66 us
  Pallas kernels: 50.2 us -> 49.2 us
    dynamic_slice x1 -> x0, local copies, waits for them, and re-layouts: 5.52 us -> none  [local(): lax.dynamic_index_in_dim(observed[0], view_order[u].astype(jnp.uint32), 0...]
    unnamed x3 -> x1, local copies, waits for them, and re-layouts: 3.34 us -> 1.8 us
    concatenate x1 -> x0, other arithmetic: 1.32 us -> none  [local(): jnp.concatenate([view_order, psf_list.reshape(12), tissue, neighbours.res...]
    slice x1 -> x0, local copies, waits for them, and re-layouts: 1.31 us -> none  [local(): view_order[u].astype(jnp.uint32)]
    pallas_call x1, Pallas kernels: 50.2 us -> 49.2 us  [whole_call(): pl.pallas_call(whole_kernel, out_shape=jax.ShapeDtypeStruct((FLAT, 128),...]
    reshape x2 -> x0, local copies, waits for them, and re-layouts: 0.7 us -> none  [the longest x1 0.62 us: local(): psf_blend.reshape(12)]
where the time goes in v4:
time: 51.9 us; the launch traced here: 51.7 us
  Pallas kernels  49.2 us (95%)
  local copies, waits for them, and re-layouts  1.8 us (3%)
  between operations  0.66 us (1%)
    pallas_call x1, Pallas kernels, whole_call(): pl.pallas_call(whole_kernel, out_shape=jax.ShapeDtypeStruct((FLAT, 128),...  49.2 us
    unnamed x1, local copies, waits for them, and re-layouts  1.8 us

profile of v4, /device:TPU:0, one launch (start us, length us, event | category | flops | bytes accessed | tf_op | source)
XLA Modules:
  0.0 51.7 jit_solution(9027188748100397023)
XLA Ops:
  0.7 49.2 %whole.1 = f32[864,128]{1,0:T(8,128)} custom-call(s32[6]{0:T(128)} %refs_0_.1, s32[2,6]{1,0:T(2,128)} %bitcast.15, f32[2,6]{1,0:T(2,128)} %bitcast.16, s32[1]{0:T(128)S(6)} %copy.20.refs_3_, s32[1,6]{1,0:T(1,128)} %refs_4_.1, f32[864,128]{1,0:T(8,128)} %bitcast.13, f32[6,1,4913]{2,1,0:T(1,128)} %bitcast.14, s32[1,128]{1,0:T(1,128)} %bitcast.17, ...), custom_call_target="tpu_custom_call" | custom-call | tf_op jit(solution)/shard_map/whole/pallas_call | solution.py:664
  49.9 1.8 %copy.21 = f32[1,110592]{1,0:T(1,128)} copy(f32[1,110592]{1,0:T(1,128)} %bitcast.11) | data formatting | bytes 884736

commit v5 on v4

--- a/solution.py
+++ b/solution.py
@@ -197,7 +197,7 @@
     return store
 
 
-def prepare(order_ref, list_ref, blend_ref, est_ref, cells_ref, pack_ref, cp_ref, weights_ref, own_ref, faces, flat_ref):
+def prepare_cells(order_ref, list_ref, blend_ref, cells_ref, weights_ref, own_ref):
     number = lax.broadcasted_iota(jnp.int32, (1, 128), 1)
     weights_ref[...] = jnp.zeros_like(weights_ref)
     own_ref[...] = jnp.zeros_like(own_ref)
@@ -214,8 +214,11 @@
         tail = KS3 // 128 * 128
         i = KS3 // 128
         own_ref[u, i : i + 1, 0 : KS3 - tail] = cells_ref[view, :, tail:KS3]
-    flat_to_pairs(load_flat(est_ref), store_rows(flat_ref))
-    cp_ref[...] = flat_ref[...].reshape(HALF, E, 128)
+
+
+def prepare_block(est_ref, pack_ref, cp_ref, faces):
+    row_ref = cp_ref.reshape(HALF * E, 128)
+    flat_to_pairs(load_flat(est_ref), store_rows(row_ref))
     emit_faces(cp_ref, pack_ref, faces)
 
 
@@ -453,15 +456,16 @@
         total = jnp.sum(jnp.sum(cell, axis=0, keepdims=True), axis=1, keepdims=True)
         scaled_ref[a] = cell / total
 
-    def body(dest, carry):
-        share = jnp.sum(weights_ref[dest, u : u + 1, :] * pick, axis=1, keepdims=True)
-        total = share[0:1, :] * scaled_ref[0]
-        for a in range(1, NEAR):
-            total = total + share[a : a + 1, :] * scaled_ref[a]
-        parts_ref[dest] = total
-        return carry
-
-    lax.fori_loop(0, FAR, body, 0)
+    def body(it, carry):
+        for dest in [it * 8 + j for j in range(8)]:
+            share = jnp.sum(weights_ref[dest, u : u + 1, :] * pick, axis=1, keepdims=True)
+            total = share[0:1, :] * scaled_ref[0]
+            for a in range(1, NEAR):
+                total = total + share[a : a + 1, :] * scaled_ref[a]
+            parts_ref[dest] = total
+        return carry
+
+    lax.fori_loop(0, FAR // 8, body, 0)
 
 
 def whole_kernel(*refs):
@@ -472,7 +476,7 @@
     load_sem = refs[6 + 2 * INPUTS]
     refs = refs[7 + 2 * INPUTS :]
     loads = [pltpu.make_async_copy(inputs[i], local_refs[i], load_sem.at[i]) for i in range(INPUTS)]
-    est_ref, cells_ref, cell_row_ref, pack_ref, seen_in, place_ref = local_refs[:6]
+    cells_ref, est_ref, pack_ref, cell_row_ref, seen_in, place_ref = local_refs[:6]
     fwd_z_ref, fwd_y_ref, tap_z_ref, tap_y_ref, inv_y_ref, inv_z_ref, fwd_yc_ref = local_refs[6:]
     for load in loads:
         load.start()
@@ -494,22 +498,9 @@
     for peer in near + far + across:
         pl.semaphore_signal(barrier, inc=1, device_id=(peer,), device_id_type=MESH)
 
+    loads[0].wait()
+    prepare_cells(order_ref, list_ref, blend_ref, cells_ref, weights_ref, own_ref)
     taps_ref[...] = jnp.zeros_like(taps_ref)
-    for load in loads[:4]:
-        load.wait()
-    prepare(
-        order_ref,
-        list_ref,
-        blend_ref,
-        est_ref,
-        cells_ref,
-        pack_ref,
-        cp_refs[0],
-        weights_ref,
-        own_ref,
-        faces[0],
-        row_ref,
-    )
     pl.semaphore_wait(barrier, len(near + far + across))
 
     near_copies = [
@@ -548,7 +539,6 @@
             copy.wait()
 
     base = me // NEAR * NEAR
-    pick = (cell_row_ref[...] == base + lax.broadcasted_iota(jnp.int32, (NEAR, 128), 0)).astype(F32)
 
     def widen(it, carry):
         for j in range(8):
@@ -565,7 +555,6 @@
         flat_to_pairs(load, store_rows(row_ref))
 
     def spectra(u):
-        wait(far_copies[u])
         total = parts[u][me // NEAR]
         for s in range(FAR - 1):
             total = total + held[u][s]
@@ -579,24 +568,30 @@
 
     start(near_copies[0])
     start(share_copies)
+    for load in loads[1:3]:
+        load.wait()
+    prepare_block(est_ref, pack_ref, cp_refs[0], faces[0])
     start(face_copies[0])
-    start(near_copies[1])
-    for load in loads[4:]:
+    for load in loads[3:]:
         load.wait()
+    pick = (cell_row_ref[...] == base + lax.broadcasted_iota(jnp.int32, (NEAR, 128), 0)).astype(F32)
     lax.fori_loop(0, FLAT // 8, widen, 0)
-    seen_pairs(0)
     wait(near_copies[0])
     wait(share_copies)
     blend_cells(0, near_all[0], weights_all, pick, scaled_ref, parts[0])
     start(far_copies[0])
+    start(near_copies[1])
+    seen_pairs(0)
     padded_spectra(0)
     wait(near_copies[1])
     blend_cells(1, near_all[1], weights_all, pick, scaled_ref, parts[1])
+    wait(far_copies[0])
     start(far_copies[1])
     spectra(0)
     correct(tissue_ref, cp_refs[0], cp_refs[1], flat_ref, tables, work)
     emit_faces(cp_refs[1], pack_ref, faces[1])
     start(face_copies[1])
+    wait(far_copies[1])
     spectra(1)
     seen_pairs(1)
     padded_spectra(1)
@@ -618,10 +613,10 @@
 
 def whole_call(scalars, est, cells, cell_row, seen):
     inputs = [
+        cells,
         est,
-        cells,
+        jnp.asarray(TABLES["pack"]),
         cell_row,
-        jnp.asarray(TABLES["pack"]),
         seen,
         jnp.asarray(TABLES["place"]),
         jnp.asarray(TABLES["fwd_z"]),

time: 51.9 us -> 50.8 us (0.979)
  Pallas kernels: 49.2 us -> 48.1 us
    pallas_call x1, Pallas kernels: 49.2 us -> 48.1 us  [whole_call(): pl.pallas_call(whole_kernel, out_shape=jax.ShapeDtypeStruct((FLAT, 128),...]
where the time goes in v5:
time: 50.8 us; the launch traced here: 50.6 us
  Pallas kernels  48.1 us (95%)
  local copies, waits for them, and re-layouts  1.8 us (4%)
  between operations  0.66 us (1%)
    pallas_call x1, Pallas kernels, whole_call(): pl.pallas_call(whole_kernel, out_shape=jax.ShapeDtypeStruct((FLAT, 128),...  48.1 us
    unnamed x1, local copies, waits for them, and re-layouts  1.8 us

profile of v5, /device:TPU:0, one launch (start us, length us, event | category | flops | bytes accessed | tf_op | source)
XLA Modules:
  0.0 50.6 jit_solution(18431399314477917582)
XLA Ops:
  0.7 48.1 %whole.1 = f32[864,128]{1,0:T(8,128)} custom-call(s32[6]{0:T(128)} %refs_0_.1, s32[2,6]{1,0:T(2,128)} %bitcast.15, f32[2,6]{1,0:T(2,128)} %bitcast.16, s32[1]{0:T(128)S(6)} %copy.20.refs_3_, s32[1,6]{1,0:T(1,128)} %refs_4_.1, f32[6,1,4913]{2,1,0:T(1,128)} %bitcast.14, f32[864,128]{1,0:T(8,128)} %bitcast.13, bf16[2,1024,128]{2,1,0:T(8,128)(2,1)} %constant.18.clone.refs_7_, ...), custom_call_target="tpu_custom_call" | custom-call | tf_op jit(solution)/shard_map/whole/pallas_call | solution.py:659
  48.8 1.8 %copy.21 = f32[1,110592]{1,0:T(1,128)} copy(f32[1,110592]{1,0:T(1,128)} %bitcast.11) | data formatting | bytes 884736

commit v6 on v5

--- a/solution.py
+++ b/solution.py
@@ -41,7 +41,7 @@
 
 def row_table(table):
     hi, lo = split_np(table)
-    return np.concatenate([hi, hi, lo, lo], axis=1)
+    return np.concatenate([hi, hi, lo], axis=1)
 
 
 def make_tables():
@@ -51,16 +51,17 @@
     cos, sin = np.cos(ang), np.sin(ang)
     fwd_z = np.block([[cos, -sin], [sin, cos]])
     inv_z = np.block([[cos, sin], [-sin, cos]]) / PAD
-    fwd_y = np.concatenate([cos, sin], axis=0)
-    inv_y = np.concatenate([cos[MARGIN : MARGIN + E], sin[MARGIN : MARGIN + E]], axis=0) / PAD
+    half = (np.arange(PAD // 2)[:, None] + 0.5) * step
+    fwd_y = np.concatenate([np.cos(half * k), np.sin(half * k)], axis=0)
+    core = k[MARGIN : MARGIN + E]
+    inv_y = np.concatenate([np.cos(half * core), np.sin(half * core)], axis=0).T / PAD
     t = np.arange(KS) - MARGIN
     ang_t = (t[:, None] * k[None, :]) % PAD * step
     tap_z = np.zeros((128, 128))
     tap_z[:KS, :PAD] = np.cos(ang_t)
     tap_z[:KS, PAD:] = -np.sin(ang_t)
-    tap_y = np.zeros((128, TAPROWS))
-    tap_y[:PAD, :KS] = np.cos(ang_t).T
-    tap_y[PAD:, :KS] = np.sin(ang_t).T
+    tap_y = np.zeros((PAD, TAPROWS))
+    tap_y[:, :KS] = np.concatenate([np.cos(half * t), np.sin(half * t)], axis=0)
     pack = np.zeros((2, 8 * 128, 128), np.float32)
     place = np.zeros((2, 128, 8 * 128), np.float32)
     for p in range(8):
@@ -110,23 +111,34 @@
     return both[:, :128] + both[:, 128:]
 
 
-def rows_dft(planes, table, count, inverse):
-    sign = lane_sign((count, 128))
-    if inverse:
-        sign = -sign
+def rows_dot(planes, table):
     out = []
     for a in range(0, len(planes), 2):
         cols = []
         for plane in planes[a : a + 2]:
             hi, lo = split(plane)
-            cols.append(jnp.concatenate([hi, lo, hi, lo], axis=0))
-        rhs = jnp.concatenate(cols, axis=1) if len(cols) > 1 else cols[0]
-        both = dot(table, rhs)
-        for b in range(len(cols)):
-            c_part = both[:count, b * 128 : (b + 1) * 128]
-            s_part = both[count : 2 * count, b * 128 : (b + 1) * 128]
-            out.append(c_part + sign * pltpu.roll(s_part, 64, 1))
+            cols.append(jnp.concatenate([hi, lo, hi], axis=0))
+        both = dot(table, jnp.concatenate(cols, axis=1) if len(cols) > 1 else cols[0])
+        out += [both[:, b * 128 : (b + 1) * 128] for b in range(len(cols))]
     return out
+
+
+def rows_forward(planes, table):
+    sign = lane_sign((PAD // 2, 128))
+    out = []
+    for both in rows_dot(planes, table):
+        turned = sign * pltpu.roll(both[PAD // 2 :], 64, 1)
+        out.append((both[: PAD // 2] + turned, both[: PAD // 2] - turned))
+    return out
+
+
+def rows_inverse(planes, table):
+    sign = -lane_sign((PAD // 2, 128))
+    folded = []
+    for plane in planes:
+        plus, minus = plane[: PAD // 2], plane[PAD // 2 :]
+        folded.append(jnp.concatenate([plus + minus, sign * pltpu.roll(plus - minus, 64, 1)], axis=0))
+    return rows_dot(folded, table)
 
 
 def emit_faces(cp_ref, pack_ref, faces):
@@ -234,8 +246,9 @@
 
     def y_body(it, carry):
         planes = [z_ref[it * group + j, 0:rows, :] for j in range(group)]
-        for j, plane in enumerate(rows_dft(planes, fwd_y_ref[...], PAD, False)):
-            spec_ref[it * group + j] = plane
+        for j, (plus, minus) in enumerate(rows_forward(planes, fwd_y_ref[...])):
+            spec_ref[it * group + j, 0 : PAD // 2, :] = plus
+            spec_ref[it * group + j, PAD // 2 : PAD, :] = minus
         return carry
 
     lax.fori_loop(0, PLANES // group, y_body, 0)
@@ -278,7 +291,7 @@
 
     def y_body(it, carry):
         planes = [spec_ref[it * group + j] for j in range(group)]
-        for j, plane in enumerate(rows_dft(planes, inv_y_ref[...], E, True)):
+        for j, plane in enumerate(rows_inverse(planes, inv_y_ref[...])):
             y_ref[it * group + j, 0:E, :] = plane
         return carry
 
@@ -301,14 +314,15 @@
             more = pltpu.roll(flat_ref[i + 1 : i + 2, :], (-at) % 128, 1)
             run = jnp.where(lane < 128 - at, run, more)
         taps_ref[r // KS, r % KS : r % KS + 1, :] = run
-    low_full = low_lanes((PAD, 128))
+    low = low_lanes((PAD // 2, 128))
     rows = lanes_dft(taps_ref[...].reshape(KS * TAPROWS, 128), tap_z_ref[...])
     z_ref[0:KS, 0:TAPROWS, :] = rows.reshape(KS, TAPROWS, 128)
     planes = [z_ref[d, 0:TAPROWS, :] for d in range(KS)]
-    for d, spec in enumerate(rows_dft(planes, tap_y_ref[...], PAD, False)):
-        other = pltpu.roll(spec, 64, 1)
-        kr_ref[d] = jnp.where(low_full, spec, other)
-        ki_ref[d] = jnp.where(low_full, other, spec)
+    for d, specs in enumerate(rows_forward(planes, tap_y_ref[...])):
+        for h, spec in enumerate(specs):
+            other = pltpu.roll(spec, 64, 1)
+            kr_ref[d, h * 32 : h * 32 + 32, :] = jnp.where(low, spec, other)
+            ki_ref[d, h * 32 : h * 32 + 32, :] = jnp.where(low, other, spec)
 
 
 def assemble(next_ref, cp_ref, halos, place_ref, ext_ref, pp_ref):
@@ -385,7 +399,7 @@
 
 def fwd_y_core():
     full = TABLES["fwd_y"]
-    return np.concatenate([full[:, s * PAD + MARGIN : s * PAD + MARGIN + E] for s in range(4)], axis=1)
+    return np.concatenate([full[:, s * PAD + MARGIN : s * PAD + MARGIN + E] for s in range(3)], axis=1)
 
 
 GRID = (4, 4, 8)

time: 50.8 us -> 49.8 us (0.980)
  Pallas kernels: 48.1 us -> 47.2 us
    pallas_call x1, Pallas kernels: 48.1 us -> 47.2 us  [whole_call(): pl.pallas_call(whole_kernel, out_shape=jax.ShapeDtypeStruct((FLAT, 128),...]
where the time goes in v6:
time: 49.8 us; the launch traced here: 49.6 us
  Pallas kernels  47.2 us (95%)
  local copies, waits for them, and re-layouts  1.8 us (4%)
  between operations  0.66 us (1%)
    pallas_call x1, Pallas kernels, whole_call(): pl.pallas_call(whole_kernel, out_shape=jax.ShapeDtypeStruct((FLAT, 128),...  47.2 us
    unnamed x1, local copies, waits for them, and re-layouts  1.8 us

profile of v6, /device:TPU:0, one launch (start us, length us, event | category | flops | bytes accessed | tf_op | source)
XLA Modules:
  0.0 49.6 jit_solution(6559806017208961135)
XLA Ops:
  0.7 47.2 %whole.1 = f32[864,128]{1,0:T(8,128)} custom-call(s32[6]{0:T(128)} %refs_0_.1, s32[2,6]{1,0:T(2,128)} %bitcast.15, f32[2,6]{1,0:T(2,128)} %bitcast.16, s32[1]{0:T(128)S(6)} %copy.20.refs_3_, s32[1,6]{1,0:T(1,128)} %refs_4_.1, f32[6,1,4913]{2,1,0:T(1,128)} %bitcast.14, f32[864,128]{1,0:T(8,128)} %bitcast.13, bf16[2,1024,128]{2,1,0:T(8,128)(2,1)} %constant.18.clone.refs_7_, ...), custom_call_target="tpu_custom_call" | custom-call | tf_op jit(solution)/shard_map/whole/pallas_call | solution.py:673
  47.8 1.8 %copy.21 = f32[1,110592]{1,0:T(1,128)} copy(f32[1,110592]{1,0:T(1,128)} %bitcast.11) | data formatting | bytes 884736

commit v7 on v6

--- a/solution.py
+++ b/solution.py
@@ -62,16 +62,16 @@
     tap_z[:KS, PAD:] = -np.sin(ang_t)
     tap_y = np.zeros((PAD, TAPROWS))
     tap_y[:, :KS] = np.concatenate([np.cos(half * t), np.sin(half * t)], axis=0)
-    pack = np.zeros((2, 8 * 128, 128), np.float32)
-    place = np.zeros((2, 128, 8 * 128), np.float32)
+    pack = np.zeros((8 * 128, 256), np.float32)
+    place = np.zeros((256, 8 * 128), np.float32)
     for p in range(8):
         for s in range(2):
             for z in range(MARGIN):
                 slot = p * 16 + s * 8 + z
-                pack[0, p * 128 + s * 64 + MARGIN + z, slot] = 1
-                pack[1, p * 128 + s * 64 + E + z, slot] = 1
-                place[0, slot, p * 128 + s * 64 + z] = 1
-                place[1, slot, p * 128 + s * 64 + MARGIN + E + z] = 1
+                pack[p * 128 + s * 64 + MARGIN + z, slot] = 1
+                pack[p * 128 + s * 64 + E + z, 128 + slot] = 1
+                place[slot, p * 128 + s * 64 + z] = 1
+                place[128 + slot, p * 128 + s * 64 + MARGIN + E + z] = 1
     return dict(
         fwd_z=lane_table(fwd_z),
         inv_z=lane_table(inv_z),
@@ -143,6 +143,12 @@
 
 def emit_faces(cp_ref, pack_ref, faces):
     xm_ref, xp_ref, ym_ref, yp_ref, zm_ref, zp_ref = faces
+    wide = [
+        jnp.concatenate([cp_ref[g * 8 + p].astype(BF16) for p in range(8)], axis=1) for g in range(3)
+    ]
+    both = dot(jnp.concatenate(wide, axis=0), pack_ref[...])
+    zm_ref[...] = both[:, :128].astype(BF16)
+    zp_ref[...] = both[:, 128:].astype(BF16)
     low = low_lanes((E, 128))
     for j in range(4):
         near = jnp.where(low, cp_ref[j], pltpu.roll(cp_ref[4 + j], 64, 1))
@@ -151,11 +157,6 @@
         xp_ref[j * E : (j + 1) * E, :] = near.astype(BF16)
     ym_ref[...] = cp_ref[:, 0:8, :].reshape(HALF * 8, 128).astype(BF16)
     yp_ref[...] = cp_ref[:, E - 8 : E, :].reshape(HALF * 8, 128).astype(BF16)
-    for g in range(3):
-        wide = jnp.concatenate([cp_ref[g * 8 + p].astype(BF16) for p in range(8)], axis=1)
-        zm_ref[g * E : (g + 1) * E, :] = dot(wide, pack_ref[0]).astype(BF16)
-        zp_ref[g * E : (g + 1) * E, :] = dot(wide, pack_ref[1]).astype(BF16)
-
 
 FACE_SHAPES = [(4 * E, 128), (4 * E, 128), (HALF * 8, 128), (HALF * 8, 128), (3 * E, 128), (3 * E, 128)]
 
@@ -235,7 +236,7 @@
 
 
 def forward_planes(src_ref, z_ref, spec_ref, rows, fwd_z_ref, fwd_y_ref):
-    group = 20
+    group = PLANES
 
     def z_body(it, carry):
         block = src_ref[pl.ds(it * group, group)].reshape(group * rows, 128)
@@ -335,14 +336,11 @@
 
     ext_ref[:, 0:8, :] = face(hym_ref, 2).reshape(HALF, 8, 128)
     ext_ref[:, 56:64, :] = face(hyp_ref, 3).reshape(HALF, 8, 128)
-    zm_all = face(hzm_ref, 4).astype(BF16)
-    zp_all = face(hzp_ref, 5).astype(BF16)
+    both = jnp.concatenate([face(hzm_ref, 4).astype(BF16), face(hzp_ref, 5).astype(BF16)], axis=1)
+    margins = dot(both, place_ref[...])
     for g in range(3):
-        zm = dot(zm_all[g * E : (g + 1) * E], place_ref[0])
-        zp = dot(zp_all[g * E : (g + 1) * E], place_ref[1])
         for p in range(8):
-            lanes = slice(p * 128, (p + 1) * 128)
-            ext_ref[g * 8 + p, 8:56, :] = cp_ref[g * 8 + p] + zm[:, lanes] + zp[:, lanes]
+            ext_ref[g * 8 + p, 8:56, :] = cp_ref[g * 8 + p] + margins[g * E : (g + 1) * E, p * 128 : (p + 1) * 128]
     xm = face(hxm_ref, 0).reshape(4, E, 128)
     xp = face(hxp_ref, 1).reshape(4, E, 128)
     pp_ref[8:32] = ext_ref[...]
@@ -532,7 +530,7 @@
     face_copies = [
         [
             remote(faces[u][f], halos[u][f ^ 1], face_send.at[u, f], face_recv.at[u, f], across[f])
-            for f in range(6)
+            for f in (4, 5, 0, 1, 2, 3)
         ]
         for u in range(UPDATES)
     ]
@@ -672,7 +670,7 @@
     scratch += [DMA((2, FAR - 1)), DMA((2, FAR - 1)), DMA((2, 6)), DMA((2, 6))]
     return pl.pallas_call(
         whole_kernel,
-        out_shape=jax.ShapeDtypeStruct((FLAT, 128), F32),
+        out_shape=pltpu.VMEM((FLAT, 128), F32),
         in_specs=[SMEM] * 5 + [pl.BlockSpec(memory_space=pl.ANY)] * INPUTS,
         out_specs=VMEM,
         scratch_shapes=scratch,

time: 49.8 us -> 46.3 us (0.930)
  Pallas kernels: 47.2 us -> 44.7 us
  local copies, waits for them, and re-layouts: 1.8 us -> 0.76 us
    pallas_call x1, Pallas kernels: 47.2 us -> 44.7 us  [whole_call(): pl.pallas_call(whole_kernel, out_shape=pltpu.VMEM((FLAT, 128), F32), in_s...]
    unnamed x1, local copies, waits for them, and re-layouts: 1.8 us -> 0.76 us
where the time goes in v7:
time: 46.3 us; the launch traced here: 46.1 us
  Pallas kernels  44.7 us (97%)
  local copies, waits for them, and re-layouts  0.76 us (2%)
  between operations  0.66 us (1%)
    pallas_call x1, Pallas kernels, whole_call(): pl.pallas_call(whole_kernel, out_shape=pltpu.VMEM((FLAT, 128), F32), in_s...  44.7 us

profile of v7, /device:TPU:0, one launch (start us, length us, event | category | flops | bytes accessed | tf_op | source)
XLA Modules:
  0.0 46.1 jit_solution(797063738234820904)
XLA Ops:
  0.7 44.7 %whole.1 = f32[864,128]{1,0:T(8,128)S(1)} custom-call(s32[6]{0:T(128)} %refs_0_.1, s32[2,6]{1,0:T(2,128)} %bitcast.15, f32[2,6]{1,0:T(2,128)} %bitcast.16, s32[1]{0:T(128)S(6)} %copy.21.refs_3_, s32[1,6]{1,0:T(1,128)} %refs_4_.1, f32[6,1,4913]{2,1,0:T(1,128)} %bitcast.14, f32[864,128]{1,0:T(8,128)} %bitcast.13, bf16[1024,256]{1,0:T(8,128)(2,1)} %constant.18.clone.refs_7_, ...), custom_call_target="tpu_custom_call" | custom-call | tf_op jit(solution)/shard_map/whole/pallas_call | solution.py:671
  45.4 0.8 %copy.20 = f32[1,110592]{1,0:T(1,128)} copy(f32[1,110592]{1,0:T(1,128)S(1)} %bitcast.11) | data formatting | bytes 884736

commit v8 on v7

--- a/solution.py
+++ b/solution.py
@@ -429,13 +429,17 @@
 FAR = 16
 
 
+NEAR_ORDER = (4, 3, 5, 2, 6, 1, 7)
+FAR_ORDER = (10, 6, 14, 9, 11, 5, 7, 13, 15, 2, 8, 1, 3, 4, 12)
+
+
 def near_peers(me):
     base = me // NEAR * NEAR
-    return [base + (me % NEAR + s) % NEAR for s in range(1, NEAR)]
+    return [base + (me % NEAR + s) % NEAR for s in NEAR_ORDER]
 
 
 def far_peers(me):
-    return [(me // NEAR + s) % FAR * NEAR + me % NEAR for s in range(1, FAR)]
+    return [(me // NEAR + s) % FAR * NEAR + me % NEAR for s in FAR_ORDER]
 
 
 def face_peers(me):
@@ -530,13 +534,13 @@
     face_copies = [
         [
             remote(faces[u][f], halos[u][f ^ 1], face_send.at[u, f], face_recv.at[u, f], across[f])
-            for f in (4, 5, 0, 1, 2, 3)
+            for f in (4, 5, 2, 3, 0, 1)
         ]
         for u in range(UPDATES)
     ]
     far_copies = [
         [
-            remote(parts[u].at[(me // NEAR + 1 + s) % FAR], held[u].at[s], far_send.at[u, s], far_recv.at[u, s], peer)
+            remote(parts[u].at[(me // NEAR + FAR_ORDER[s]) % FAR], held[u].at[s], far_send.at[u, s], far_recv.at[u, s], peer)
             for s, peer in enumerate(far)
         ]
         for u in range(UPDATES)

time: 46.3 us -> 46.2 us (level)
  no operation moved by 1% of the time
where the time goes in v8:
time: 46.2 us; the launch traced here: 46.1 us
  Pallas kernels  44.7 us (97%)
  local copies, waits for them, and re-layouts  0.76 us (2%)
  between operations  0.66 us (1%)
    pallas_call x1, Pallas kernels, whole_call(): pl.pallas_call(whole_kernel, out_shape=pltpu.VMEM((FLAT, 128), F32), in_s...  44.7 us

profile of v8, /device:TPU:0, one launch (start us, length us, event | category | flops | bytes accessed | tf_op | source)
XLA Modules:
  0.0 46.1 jit_solution(7429404333126834733)
XLA Ops:
  0.7 44.7 %whole.1 = f32[864,128]{1,0:T(8,128)S(1)} custom-call(s32[6]{0:T(128)} %refs_0_.1, s32[2,6]{1,0:T(2,128)} %bitcast.15, f32[2,6]{1,0:T(2,128)} %bitcast.16, s32[1]{0:T(128)S(6)} %copy.21.refs_3_, s32[1,6]{1,0:T(1,128)} %refs_4_.1, f32[6,1,4913]{2,1,0:T(1,128)} %bitcast.14, f32[864,128]{1,0:T(8,128)} %bitcast.13, bf16[1024,256]{1,0:T(8,128)(2,1)} %constant.18.clone.refs_7_, ...), custom_call_target="tpu_custom_call" | custom-call | tf_op jit(solution)/shard_map/whole/pallas_call | solution.py:675
  45.3 0.8 %copy.20 = f32[1,110592]{1,0:T(1,128)} copy(f32[1,110592]{1,0:T(1,128)S(1)} %bitcast.11) | data formatting | bytes 884736

commit v9 on v8

--- a/solution.py
+++ b/solution.py
@@ -212,8 +212,6 @@
 
 def prepare_cells(order_ref, list_ref, blend_ref, cells_ref, weights_ref, own_ref):
     number = lax.broadcasted_iota(jnp.int32, (1, 128), 1)
-    weights_ref[...] = jnp.zeros_like(weights_ref)
-    own_ref[...] = jnp.zeros_like(own_ref)
     for u in range(UPDATES):
         view = order_ref[u]
         first = jnp.full((1, 128), blend_ref[0, view], F32)
@@ -514,9 +512,11 @@
     for peer in near + far + across:
         pl.semaphore_signal(barrier, inc=1, device_id=(peer,), device_id_type=MESH)
 
+    weights_ref[...] = jnp.zeros_like(weights_ref)
+    own_ref[...] = jnp.zeros_like(own_ref)
+    taps_ref[...] = jnp.zeros_like(taps_ref)
     loads[0].wait()
     prepare_cells(order_ref, list_ref, blend_ref, cells_ref, weights_ref, own_ref)
-    taps_ref[...] = jnp.zeros_like(taps_ref)
     pl.semaphore_wait(barrier, len(near + far + across))
 
     near_copies = [

time: 46.2 us -> 46.2 us (level)
  no operation moved by 1% of the time
where the time goes in v9:
time: 46.2 us; the launch traced here: 46.1 us
  Pallas kernels  44.7 us (97%)
  local copies, waits for them, and re-layouts  0.76 us (2%)
  between operations  0.66 us (1%)
    pallas_call x1, Pallas kernels, whole_call(): pl.pallas_call(whole_kernel, out_shape=pltpu.VMEM((FLAT, 128), F32), in_s...  44.7 us

profile of v9, /device:TPU:0, one launch (start us, length us, event | category | flops | bytes accessed | tf_op | source)
XLA Modules:
  0.0 46.1 jit_solution(16981783497956426581)
XLA Ops:
  0.7 44.7 %whole.1 = f32[864,128]{1,0:T(8,128)S(1)} custom-call(s32[6]{0:T(128)} %refs_0_.1, s32[2,6]{1,0:T(2,128)} %bitcast.15, f32[2,6]{1,0:T(2,128)} %bitcast.16, s32[1]{0:T(128)S(6)} %copy.21.refs_3_, s32[1,6]{1,0:T(1,128)} %refs_4_.1, f32[6,1,4913]{2,1,0:T(1,128)} %bitcast.14, f32[864,128]{1,0:T(8,128)} %bitcast.13, bf16[1024,256]{1,0:T(8,128)(2,1)} %constant.18.clone.refs_7_, ...), custom_call_target="tpu_custom_call" | custom-call | tf_op jit(solution)/shard_map/whole/pallas_call | solution.py:675
  45.3 0.8 %copy.20 = f32[1,110592]{1,0:T(1,128)} copy(f32[1,110592]{1,0:T(1,128)S(1)} %bitcast.11) | data formatting | bytes 884736
